TPU v7x, 512 devices: a whole 4x8x8 slice. The times are simulated.
512 devices in a mesh: fix: 64 (over z, x, core), subj: 8 (over y).
Axes of the slice: x: 4, y: 8, z: 8, core: 2. Of those that a mesh axis runs over, the one named last changes fastest.
Arguments:
- fixels: float32 [65536, 1024], P('fix', 'subj'), may hold values from -6 to 6
- conn_tiles: float32 [512, 4, 128, 128], P('fix'), may hold values from -0.25 to 0.25
- columns: int32 [512, 4], P('fix'), may hold values from 0 to 511, as said below
- nuisance: float32 [4, 1024], P(None, 'subj'), may hold values from -5 to 5
- nuisance_pinv: float32 [4, 1024], P(None, 'subj'), may hold values from -0.1875 to 0.1875
- contrast: float32 [4, 1024], replicated, may hold values from -0.1875 to 0.1875
- perm_table: int32 [128, 1024], P(None, 'subj'), may hold values from 0 to 1023, each once within a row
Outputs:
- projections: float32 [512, 65536], P('subj', 'fix')
Inputs may be any that keep to these rules, and one draw needn't show every extreme that they name: `columns`: device j of fix holds blocks j * 8 to (j + 1) * 8 - 1. The 32 entries of one device's rows name blocks of any one device at most 1 times, and in every draw some device's blocks are named exactly 1 times by the rows of every device. `perm_table`: each row is a permutation of the 1024 subjects.
All inputs are finite; a program needn't handle non-finite values.
Results may differ from a plain program's by a relative error of at most 0.000071.
Values sent between devices are 32-bit elements; how exact they have to be, the bound alone decides.
A program may use at most 64 MiB of HBM per device.

v0:
```python
import jax
import jax.numpy as jnp
from jax import lax
from jax.sharding import PartitionSpec as P


def design_rows(contrast, perm_table):
    picked = jnp.take(contrast, perm_table, axis=1)
    return jnp.transpose(picked, (1, 0, 2)).reshape(-1, perm_table.shape[1])


def per_device(fixels, conn_tiles, columns, nuisance, nuisance_pinv, contrast, perm_table):
    fix_count = lax.axis_size("fix")
    block_count, per_row = columns.shape
    block_size = conn_tiles.shape[2]
    subj_count = fixels.shape[1]
    tile_total = block_count * per_row
    wanted = columns.reshape(tile_total)
    owners = wanted // block_count
    local_index = wanted % block_count
    capacity = (tile_total + fix_count - 1) // fix_count
    positions = jnp.arange(tile_total)
    earlier = positions[:, None] > positions[None, :]
    same_owner = owners[:, None] == owners[None, :]
    ranks = jnp.sum(jnp.logical_and(same_owner, earlier), axis=1)
    slots = owners * capacity + ranks
    request = jnp.zeros((fix_count * capacity,), jnp.int32).at[slots].set(local_index)
    asked = lax.all_to_all(
        request.reshape(fix_count, capacity), "fix", split_axis=0, concat_axis=0, tiled=True
    ).reshape(-1)
    design = design_rows(contrast, perm_table)
    own_blocks = fixels.reshape(block_count, block_size, subj_count)
    outgoing = jnp.take(own_blocks, asked, axis=0).reshape(
        fix_count, capacity, block_size, subj_count
    )
    arrived = lax.all_to_all(outgoing, "fix", split_axis=0, concat_axis=0, tiled=True).reshape(
        fix_count * capacity, block_size, subj_count
    )
    needed = jnp.take(arrived, slots, axis=0).reshape(block_count, per_row, block_size, subj_count)
    smoothed = jnp.einsum(
        "bkij,bkjs->bis", conn_tiles, needed, precision=lax.Precision.HIGHEST
    ).reshape(block_count * block_size, subj_count)
    fitted_part = jnp.einsum("ns,fs->nf", nuisance_pinv, smoothed, precision=lax.Precision.HIGHEST)
    fitted = lax.psum(fitted_part, "subj")
    residual = smoothed - jnp.einsum("nf,ns->fs", fitted, nuisance, precision=lax.Precision.HIGHEST)
    partial_value = jnp.einsum("cs,fs->cf", design, residual, precision=lax.Precision.HIGHEST)
    return lax.psum_scatter(partial_value, "subj", scatter_dimension=0, tiled=True)


def solution(mesh):
    placed = (
        P("fix", "subj"),
        P("fix", None, None, None),
        P("fix", None),
        P(None, "subj"),
        P(None, "subj"),
        P(),
        P(None, "subj"),
    )
    return jax.shard_map(
        per_device, mesh=mesh, in_specs=placed, out_specs=P("subj", "fix"), check_vma=False
    )
```

profile of v0, /device:TPU:1, one launch (start us, length us, event | category | flops | bytes accessed | tf_op | source)
XLA Modules:
  0.0 228.5 jit_solution(1409098919103364654)
XLA Ops:
  6.5 0.9 copy.43
  7.4 0.1 reshape.202
  7.5 0.1 reshape.203
  7.6 0.2 convert_reduce_fusion
  7.8 0.7 scatter_custom_fusion
  8.5 0.1 copy.49
  8.6 24.0 %all_to_all.20 = s32[64,1,1]{2,1,0:T(1,128)S(1)} all-to-all(s32[64,1,1]{2,1,0:T(1,128)S(1)} %copy.49), channel_id=1, replica_groups=mesh['fix'=64,'subj'=8] {'fix'}, dimensions={0} | all-to-all | bytes 512 | tf_op jit(solution)/shard_map/all_to_all | solution.py:28
  32.6 1.2 reduce
  33.9 3.8 %gather_fusion.1 = f32[64,128,128]{2,1,0:T(8,128)} fusion(f32[8,128,128]{2,1,0:T(8,128)} %bitcast.37, s32[1024]{0:T(1024)S(1)} %pad_clamp_fusion.1), kind=kCustom, calls=%fused_computation.1 | custom fusion | bytes 8388864 | tf_op jit(solution)/shard_map/jit(_take)/gather | solution.py:33
  37.7 4.5 %bitcast_select_fusion = f32[64,1,128,128]{3,2,1,0:T(8,128)} fusion(f32[64,128,128]{2,1,0:T(8,128)} %gather_fusion.1, pred[64]{0:T(512)(128)(4,1)S(1)} %compare_and_fusion.2), kind=kLoop, calls=%fused_computation.4 | loop fusion | flops 1048576 | bytes 8388672 | tf_op jit(solution)/shard_map/jit(_take)/select_n | solution.py:33
  42.2 5.8 %all-to-all-start.1 = ((f32[64,1,128,128]{3,2,1,0:T(8,128)}), f32[64,1,128,128]{3,2,1,0:T(8,128)}, u32[]{:S(2)}, u32[]{:S(2)}) async-start(f32[64,1,128,128]{3,2,1,0:T(8,128)} %bitcast_select_fusion), calls=%async_computation.1 | async-start | bytes 8388608 | tf_op jit(solution)/shard_map/all_to_all | solution.py:36
  48.1 0.1 reduce_sum.14
  48.2 0.2 copy.41
  48.4 54.4 %gather_fusion = f32[16384,4]{1,0:T(8,128)} fusion(f32[4,1024]{0,1:T(8,128)S(1)} %copy.41, s32[16384]{0:T(1024)S(1)} %bitcast_clamp_fusion), kind=kCustom, calls=%fused_computation | custom fusion | bytes 589824 | tf_op jit(solution)/shard_map/jit(_take)/gather | solution.py:8
  102.9 5.5 %copy.42 = f32[128,128,4]{1,2,0:T(4,128)S(1)} copy(f32[128,128,4]{2,1,0:T(8,128)} %bitcast.38) | data formatting | bytes 524288 | tf_op jit(solution)/shard_map/jit(_take)/gather | solution.py:8
  108.4 0.1 broadcast_select_fusion
  108.5 34.4 %all-to-all-done.1 = f32[64,1,128,128]{3,2,1,0:T(8,128)} async-done(((f32[64,1,128,128]{3,2,1,0:T(8,128)}), f32[64,1,128,128]{3,2,1,0:T(8,128)}, u32[]{:S(2)}, u32[]{:S(2)}) %all-to-all-start.1) | async-done | bytes 4194336 | tf_op jit(solution)/shard_map/all_to_all | solution.py:36
  142.9 4.2 %gather_fusion.2 = f32[32,128,128]{2,1,0:T(8,128)} fusion(f32[64,128,128]{2,1,0:T(8,128)} %bitcast.10, s32[1024]{0:T(1024)S(1)} %pad_clamp_fusion), kind=kCustom, calls=%fused_computation.2 | custom fusion | bytes 4194432 | tf_op jit(solution)/shard_map/jit(_take)/gather | solution.py:39
  147.2 4.1 %fusion = f32[8,128,128,1]{1,2,3,0:T(8,128)S(1)} fusion(f32[8,4,128,128]{3,2,1,0:T(8,128)S(1)} %copy-done, f32[8,4,128,128]{3,2,1,0:T(8,128)} %bitcast.39, pred[8,4]{1,0:T(8,128)(4,1)S(1)} %compare_and_fusion.1), kind=kOutput, calls=%fused_computation.5 | convolution fusion | flops 805830656 | bytes 4718624 | tf_op jit(solution)/shard_map/bkij,bkjs->bis/dot_general | solution.py:40
  151.3 0.5 convolution_bitcast_fusion
  151.8 23.3 %psum.7 = f32[4,1024]{1,0:T(4,128)S(1)} all-reduce(f32[4,1024]{1,0:T(4,128)S(1)} %convolution_bitcast_fusion), channel_id=1, replica_groups=mesh['fix'=64,'subj'=8] {'subj'}, use_global_device_ids=true, to_apply=%region_2.3 | all-reduce | flops 4096 | bytes 32768 | tf_op jit(solution)/shard_map/psum | solution.py:44
  175.1 1.0 convolution_subtract_fusion
  176.1 3.2 %fusion.13 = f32[512,1024]{1,0:T(8,128)} fusion(f32[512,128]{1,0:T(8,128)S(1)} %bitcast.42, f32[1024,128]{1,0:T(8,128)S(1)} %convolution_subtract_fusion), kind=kOutput, calls=%fused_computation.49 | convolution fusion | flops 805306368 | bytes 2883584 | tf_op jit(solution)/shard_map/cs,fs->cf/dot_general | solution.py:46
  179.3 42.4 %reduce-scatter.2.cloned.1.call-done = f32[64,1024]{1,0:T(8,128)} async-done(((f32[512,1024]{1,0:T(8,128)}), f32[64,1024]{1,0:T(8,128)}) %reduce-scatter.2.cloned.1.call-update) | async-done | bytes 262160 | tf_op jit(solution)/shard_map/reduce_scatter | solution.py:47
  (21 shorter events, 0.2 us)
Async XLA Ops:
  6.5 140.6 %copy-start = (f32[8,4,128,128]{3,2,1,0:T(8,128)S(1)}, f32[8,4,128,128]{3,2,1,0:T(8,128)}, u32[]{:S(2)}) copy-start(f32[8,4,128,128]{3,2,1,0:T(8,128)} %param.8) | copy-start | bytes 6291460
  42.2 6.0 %copy-start.2 = (f32[4,1024]{1,0:T(4,128)S(1)}, f32[4,1024]{1,0:T(4,128)}, u32[]{:S(2)}) copy-start(f32[4,1024]{1,0:T(4,128)} %param.12) | copy-start | bytes 49156
  42.2 6.2 %copy-start.1 = (s32[128,128]{1,0:T(8,128)S(1)}, s32[128,128]{1,0:T(8,128)}, u32[]{:S(2)}) copy-start(s32[128,128]{1,0:T(8,128)} %param.13) | copy-start | bytes 196612
  42.2 100.8 %all-to-all-start.1 = ((f32[64,1,128,128]{3,2,1,0:T(8,128)}), f32[64,1,128,128]{3,2,1,0:T(8,128)}, u32[]{:S(2)}, u32[]{:S(2)}) async-start(f32[64,1,128,128]{3,2,1,0:T(8,128)} %bitcast_select_fusion), calls=%async_computation.1 | async-start | bytes 8388608 | tf_op jit(solution)/shard_map/all_to_all | solution.py:36
  48.0 173.6 %reduce-scatter.2.cloned.1.call-start = ((), (), s32[]{:S(2)}) async-start(), calls=%async_computation.3 | async-start | bytes 2359296 | tf_op jit(solution)/shard_map/reduce_scatter | solution.py:47
  147.2 4.1 %copy-start.3 = (f32[4,128]{1,0:T(4,128)S(1)}, f32[4,128]{1,0:T(4,128)}, u32[]{:S(2)}) copy-start(f32[4,128]{1,0:T(4,128)} %param.11) | copy-start | bytes 6148
  147.2 28.0 %copy-start.4 = (f32[4,128]{1,0:T(4,128)S(1)}, f32[4,128]{1,0:T(4,128)}, u32[]{:S(2)}) copy-start(f32[4,128]{1,0:T(4,128)} %param.10) | copy-start | bytes 6148
Sparse Core Ops, SparseCore 0:
  179.4 42.2 reduce-scatter.1
where the time goes:
time: 233 us; the launch traced here: 229 us
  waiting for transfers between devices  76.8 us (33%)
  local copies, waits for them, and re-layouts  70.1 us (30%)
  blocking collectives  47.3 us (20%)
  between operations  13.5 us (6%)
  matrix products  8.82 us (4%)
  other arithmetic  6.09 us (3%)
  starting transfers between devices  5.88 us (3%)
    gather x2, local copies, waits for them, and re-layouts, design_rows(): picked = jnp.take(contrast, perm_table, axis=1)  59.9 us
    reduce_scatter x1, waiting for transfers between devices, per_device(): lax.psum_scatter(partial_value, 'subj', scatter_dimension=0, tiled=True)  42.4 us
    all_to_all x1, waiting for transfers between devices, per_device(): lax.all_to_all(outgoing, 'fix', split_axis=0, concat_axis=0, tiled=True)  34.4 us
    all_to_all x1, blocking collectives, per_device(): lax.all_to_all(request.reshape(fix_count, capacity), 'fix', split_axis=0,...  24 us
    psum x1, blocking collectives, per_device(): fitted = lax.psum(fitted_part, 'subj')  23.3 us
    all_to_all x1, starting transfers between devices, per_device(): lax.all_to_all(outgoing, 'fix', split_axis=0, concat_axis=0, tiled=True)  5.84 us
  transfers between devices with their start and end apart: 2, of which 2 were waited for; matrix products, arithmetic and copies ran while one was open for 26% of the time, Pallas kernels for 0%

commit v1 on v0

v1 whole, which is shorter than its diff:
```python
import jax
import jax.numpy as jnp
from jax import lax
from jax.sharding import PartitionSpec as P

HI = lax.Precision.HIGHEST


def design_rows(contrast, perm_table):
    picked = jnp.take(contrast, perm_table, axis=1)
    return jnp.transpose(picked, (1, 0, 2)).reshape(-1, perm_table.shape[1])


def per_device(fixels, conn_tiles, columns, nuisance, nuisance_pinv, contrast, perm_table):
    fix_count = lax.axis_size("fix")
    subj_parts = lax.axis_size("subj")
    block_count, per_row = columns.shape
    block_size = conn_tiles.shape[2]
    nuis = nuisance.shape[0]
    fixel_count = fixels.shape[0]
    tile_total = block_count * per_row
    wanted = columns.reshape(tile_total)
    owners = wanted // block_count
    local_index = wanted % block_count
    capacity = (tile_total + fix_count - 1) // fix_count
    positions = jnp.arange(tile_total)
    earlier = positions[:, None] > positions[None, :]
    same_owner = owners[:, None] == owners[None, :]
    ranks = jnp.sum(jnp.logical_and(same_owner, earlier), axis=1)
    slots = owners * capacity + ranks
    request = jnp.zeros((fix_count * capacity,), jnp.int32).at[slots].set(local_index)
    asked = lax.all_to_all(
        request.reshape(fix_count, capacity), "fix", split_axis=0, concat_axis=0, tiled=True
    ).reshape(-1)
    design = design_rows(contrast, perm_table)
    rows = design.shape[0] // subj_parts
    part = jnp.einsum("cs,fs->cf", design, fixels, precision=HI)
    fit = jnp.einsum("ns,fs->nf", nuisance_pinv, fixels, precision=HI)
    load = jnp.einsum("ns,cs->nc", nuisance, design, precision=HI)
    load = jnp.transpose(load.reshape(nuis, subj_parts, rows), (1, 0, 2))
    load = jnp.pad(load, ((0, 0), (0, 0), (0, fixel_count - rows)))
    fit = jnp.broadcast_to(fit[None], (subj_parts, nuis, fixel_count))
    stacked = jnp.concatenate([part.reshape(subj_parts, rows, fixel_count), fit, load], axis=1)
    summed = lax.psum_scatter(stacked, "subj", scatter_dimension=0, tiled=True)[0]
    own = summed[:rows] - jnp.einsum(
        "nc,nf->cf", summed[rows + nuis :, :rows], summed[rows : rows + nuis], precision=HI
    )
    own_blocks = jnp.transpose(own.reshape(rows, block_count, block_size), (1, 0, 2))
    outgoing = jnp.take(own_blocks, asked, axis=0).reshape(fix_count, capacity, rows, block_size)
    arrived = lax.all_to_all(outgoing, "fix", split_axis=0, concat_axis=0, tiled=True).reshape(
        fix_count * capacity, rows, block_size
    )
    needed = jnp.take(arrived, slots, axis=0).reshape(block_count, per_row, rows, block_size)
    out = jnp.einsum("bkcj,bkij->cbi", needed, conn_tiles, precision=HI)
    return out.reshape(rows, fixel_count)


def solution(mesh):
    placed = (
        P("fix", "subj"),
        P("fix", None, None, None),
        P("fix", None),
        P(None, "subj"),
        P(None, "subj"),
        P(),
        P(None, "subj"),
    )
    return jax.shard_map(
        per_device, mesh=mesh, in_specs=placed, out_specs=P("subj", "fix"), check_vma=False
    )
```

time: 233 us -> 206 us (0.88); the launches traced: 229 us -> 205 us
  blocking collectives: 47.3 us -> 24 us
  starting transfers between devices: 5.88 us -> 15.2 us
  waiting for transfers between devices: 76.8 us -> 69.6 us
  matrix products: 8.82 us -> 6.45 us
    psum x1 -> x0, blocking collectives: 23.3 us -> none  [per_device(): fitted = lax.psum(fitted_part, 'subj')]
    reduce_scatter x1, waiting for transfers between devices: 42.4 us -> 20 us  [per_device(): lax.psum_scatter(stacked, 'subj', scatter_dimension=0, tiled=True)[0]]
    all_to_all x1, waiting for transfers between devices: 34.4 us -> 49.5 us  [per_device(): lax.all_to_all(outgoing, 'fix', split_axis=0, concat_axis=0, tiled=True)]
    all_to_all x1, starting transfers between devices: 5.84 us -> 15.2 us  [per_device(): lax.all_to_all(outgoing, 'fix', split_axis=0, concat_axis=0, tiled=True)]
    dot_general x4 -> x5, matrix products: 8.82 us -> 6.45 us  [the longest x1 2.4 us: per_device(): out = jnp.einsum('bkcj,bkij->cbi', needed, conn_tiles, precision=HI)]
  transfers between devices with their start and end apart: 2 -> 2, of which waited for: 2 -> 2; matrix products, arithmetic and copies ran while one was open for 26% -> 1% of each run, Pallas kernels for 0% -> 0%
where the time goes in v1:
time: 206 us; the launch traced here: 205 us
  waiting for transfers between devices  69.6 us (34%)
  local copies, waits for them, and re-layouts  68.1 us (33%)
  blocking collectives  24 us (12%)
  starting transfers between devices  15.2 us (7%)
  between operations  13.6 us (7%)
  other arithmetic  8.15 us (4%)
  matrix products  6.45 us (3%)
    gather x2, local copies, waits for them, and re-layouts, design_rows(): picked = jnp.take(contrast, perm_table, axis=1)  60.3 us
    all_to_all x1, waiting for transfers between devices, per_device(): lax.all_to_all(outgoing, 'fix', split_axis=0, concat_axis=0, tiled=True)  49.5 us
    all_to_all x1, blocking collectives, per_device(): lax.all_to_all(request.reshape(fix_count, capacity), 'fix', split_axis=0,...  24 us
    reduce_scatter x1, waiting for transfers between devices, per_device(): lax.psum_scatter(stacked, 'subj', scatter_dimension=0, tiled=True)[0]  20 us
    all_to_all x1, starting transfers between devices, per_device(): lax.all_to_all(outgoing, 'fix', split_axis=0, concat_axis=0, tiled=True)  15.2 us
  transfers between devices with their start and end apart: 2, of which 2 were waited for; matrix products, arithmetic and copies ran while one was open for 1% of the time, Pallas kernels for 0%

profile of v1, /device:TPU:1, one launch (start us, length us, event | category | flops | bytes accessed | tf_op | source)
XLA Modules:
  0.0 205.0 jit_solution(13905463846953447668)
XLA Ops:
  6.5 1.0 bitcast_clamp_fusion
  7.5 0.9 compare_and_fusion
  8.4 0.9 copy.61
  9.4 54.8 %gather_fusion = f32[16384,4]{1,0:T(8,128)} fusion(f32[4,1024]{0,1:T(8,128)S(1)} %copy.61, s32[16384]{0:T(1024)S(1)} %bitcast_clamp_fusion), kind=kCustom, calls=%fused_computation | custom fusion | bytes 589824 | tf_op jit(solution)/shard_map/jit(_take)/gather | solution.py:10
  64.1 5.5 %copy.62 = f32[128,128,4]{1,2,0:T(4,128)S(1)} copy(f32[128,128,4]{2,1,0:T(8,128)} %bitcast.67) | data formatting | bytes 524288 | tf_op jit(solution)/shard_map/jit(_take)/gather | solution.py:10
  69.8 0.3 convolution_bitcast_fusion.1
  70.2 0.5 fusion.17
  70.8 1.8 fusion.3
  72.6 1.6 select_maximum_fusion
  74.2 0.7 copy-done.4
  75.2 0.2 convert_reduce_fusion
  75.4 0.7 scatter_custom_fusion
  76.0 0.1 copy.60
  76.1 24.0 %all_to_all.20 = s32[64,1,1]{2,1,0:T(1,128)S(1)} all-to-all(s32[64,1,1]{2,1,0:T(1,128)S(1)} %copy.60), channel_id=1, replica_groups=mesh['fix'=64,'subj'=8] {'fix'}, dimensions={0} | all-to-all | bytes 512 | tf_op jit(solution)/shard_map/all_to_all | solution.py:32
  100.2 1.2 reduce
  101.4 20.0 %reduce-scatter.2.cloned.1.call-done = f32[1,72,1024]{2,1,0:T(8,128)} async-done(((f32[8,72,1024]{2,1,0:T(8,128)}), f32[1,72,1024]{2,1,0:T(8,128)}) %reduce-scatter.2.cloned.1.call-update) | async-done | bytes 294928 | tf_op jit(solution)/shard_map/reduce_scatter | solution.py:44
  121.5 1.4 fusion.1
  122.9 2.0 gather_fusion.1
  124.9 3.1 %fusion = f32[64,1,64,128]{3,2,1,0:T(8,128)} fusion(f32[64,64,128]{2,1,0:T(8,128)} %gather_fusion.1, pred[64]{0:T(512)(128)(4,1)S(1)} %compare_and_fusion.2), kind=kLoop, calls=%fused_computation.7 | loop fusion | flops 524288 | bytes 4194368 | tf_op jit(solution)/shard_map/jit(_take)/select_n | solution.py:49
  128.0 15.2 %all-to-all-start.1 = ((f32[64,1,64,128]{3,2,1,0:T(8,128)}), f32[64,1,64,128]{3,2,1,0:T(8,128)}, u32[]{:S(2)}, u32[]{:S(2)}) async-start(f32[64,1,64,128]{3,2,1,0:T(8,128)} %fusion), calls=%async_computation.2 | async-start | bytes 4194304 | tf_op jit(solution)/shard_map/all_to_all | solution.py:50
  143.3 49.5 %all-to-all-done.1 = f32[64,1,64,128]{3,2,1,0:T(8,128)} async-done(((f32[64,1,64,128]{3,2,1,0:T(8,128)}), f32[64,1,64,128]{3,2,1,0:T(8,128)}, u32[]{:S(2)}, u32[]{:S(2)}) %all-to-all-start.1) | async-done | bytes 2097184 | tf_op jit(solution)/shard_map/all_to_all | solution.py:50
  192.8 2.2 %gather_fusion.2 = f32[32,64,128]{2,1,0:T(8,128)S(1)} fusion(f32[64,64,128]{2,1,0:T(8,128)} %bitcast.18, s32[1024]{0:T(1024)S(1)} %pad_clamp_fusion), kind=kCustom, calls=%fused_computation.2 | custom fusion | bytes 2097280 | tf_op jit(solution)/shard_map/jit(_take)/gather | solution.py:53
  195.0 2.4 %convolution_bitcast_fusion = f32[8,8,8,128]{3,2,1,0:T(8,128)S(1)} fusion(f32[8,4,128,128]{3,2,1,0:T(8,128)S(1)} %copy-done, f32[8,4,64,128]{3,2,1,0:T(8,128)S(1)} %bitcast.68, pred[8,4]{1,0:T(8,128)(4,1)S(1)} %compare_and_fusion.1), kind=kOutput, calls=%fused_computation.8 | convolution fusion | flops 402915328 | bytes 3407904 | tf_op jit(solution)/shard_map/bkcj,bkij->cbi/dot_general | solution.py:54
  197.4 0.7 copy.73
  (27 shorter events, 0.7 us)
Async XLA Ops:
  6.5 188.5 %copy-start = (f32[8,4,128,128]{3,2,1,0:T(8,128)S(1)}, f32[8,4,128,128]{3,2,1,0:T(8,128)}, u32[]{:S(2)}) copy-start(f32[8,4,128,128]{3,2,1,0:T(8,128)} %param.8) | copy-start | bytes 6291460
  6.5 114.9 %reduce-scatter.2.cloned.1.call-start = ((), (), s32[]{:S(2)}) async-start(), calls=%async_computation.3 | async-start | bytes 2654208 | tf_op jit(solution)/shard_map/reduce_scatter | solution.py:44
  64.1 5.7 %copy-start.2 = (f32[4,128]{1,0:T(4,128)S(1)}, f32[4,128]{1,0:T(4,128)}, u32[]{:S(2)}) copy-start(f32[4,128]{1,0:T(4,128)} %param.10) | copy-start | bytes 6148
  64.1 6.1 %copy-start.1 = (f32[1024,128]{1,0:T(8,128)S(1)}, f32[1024,128]{1,0:T(8,128)}, u32[]{:S(2)}) copy-start(f32[1024,128]{1,0:T(8,128)} %param.7) | copy-start | bytes 1572868
  64.1 6.1 %copy-start.3 = (f32[4,128]{1,0:T(4,128)S(1)}, f32[4,128]{1,0:T(4,128)}, u32[]{:S(2)}) copy-start(f32[4,128]{1,0:T(4,128)} %param.11) | copy-start | bytes 6148
  74.2 0.7 copy-start.4
  128.0 64.8 %all-to-all-start.1 = ((f32[64,1,64,128]{3,2,1,0:T(8,128)}), f32[64,1,64,128]{3,2,1,0:T(8,128)}, u32[]{:S(2)}, u32[]{:S(2)}) async-start(f32[64,1,64,128]{3,2,1,0:T(8,128)} %fusion), calls=%async_computation.2 | async-start | bytes 4194304 | tf_op jit(solution)/shard_map/all_to_all | solution.py:50
Sparse Core Ops, SparseCore 0:
  74.4 47.0 reduce-scatter.1

commit v2 on v0

v2 whole, which is shorter than its diff:
```python
import functools

import jax
import jax.numpy as jnp
from jax import lax
from jax.experimental import pallas as pl
from jax.experimental.pallas import tpu as pltpu
from jax.sharding import PartitionSpec as P

MESH = pl.DeviceIdType.MESH
F32, BF16 = jnp.float32, jnp.bfloat16
BS = 128
NX, NQ = 4, 2
ROWS = 16
EXTRA = 8
NT = (((1,), (1,)), ((), ()))
DIRECT = (2, 3, 6, 7, 1)


def plan(chunks, hy, hz, tiles, rows):
    rate, lat = 46e3, 1.8
    size = rows * BS * 4 * 8
    cost = dict(s0=0.1, a=0.2, fin=0.3, zf=0.05, xp=0.5, xf=0.05, sm=1.2, tp=0.3)
    stages = [("s0", 0)] + [("a", s) for s in range(hy - 1)] + [("fin", 0)]
    stages += [("zf", s) for s in range(hz - 1)] + [("xp", 0), ("xf", 0), ("sm", 0)]
    free = dict(y=0.0, z=0.0, x=0.0)
    at, ready = [0] * chunks, [0.0] * chunks
    order, t, prepared = [], 0.0, 0

    def send(link, amount):
        free[link] = max(free[link], t) + amount / rate
        return free[link] + lat

    while any(i < len(stages) for i in at):
        best, soonest = None, 1e9
        for c in range(chunks):
            if at[c] == len(stages):
                continue
            when = ready[c]
            if at[c] == 0:
                if c and at[c - 1] == 0:
                    continue
                when = max(when, free["y"] - 0.3)
            if stages[at[c]][0] == "sm" and prepared < tiles:
                continue
            if when <= t and best is None:
                best = c
            soonest = min(soonest, when)
        if best is None:
            if prepared < tiles and order:
                order.append(("tp", prepared, 0))
                prepared += 1
                t += cost["tp"]
            else:
                t = max(soonest, t + 1e-6)
            continue
        name, step = stages[at[best]]
        order.append((name, best, step))
        t += cost[name]
        if name == "s0":
            ready[best] = send("y", size / 2)
        elif name == "a":
            ready[best] = send("y", size)
        elif name == "fin":
            ready[best] = send("z", size)
        elif name == "zf":
            ready[best] = send("z", size if step < hz - 2 else size / 2)
        elif name == "xp":
            ready[best] = send("x", size)
            send("x", 2 * size)
        elif name == "xf":
            ready[best] = send("x", size)
        at[best] += 1
    return order


def split3(value, first):
    high = value.astype(BF16)
    low = (value - high.astype(F32)).astype(BF16)
    return [high, high, low] if first else [high, low, high]


def kernel(ny, nz, chunks, *refs):
    (x_ref, t_ref, perm_ref, con_ref, nui_ref, pinv_ref, req_ref, col_ref, out_ref), refs = refs[:9], refs[9:]
    dsc, dcat, xcat, part, gpart, mts, gfin, mcol, tv, thi, tlo, rq, rqs = refs[:13]
    refs = refs[13:]
    sb, refs = refs[:chunks], refs[chunks:]
    rb, refs = refs[:chunks], refs[chunks:]
    zb, refs = refs[:chunks], refs[chunks:]
    pk, refs = refs[:chunks], refs[chunks:]
    xr, refs = refs[:chunks], refs[chunks:]
    rl, refs = refs[:chunks], refs[chunks:]
    ys, yr, zs, zr, xs, xv, fs, fv, hs, hv, qs, qv, loc = refs
    hy, hz = ny // 2, nz // 2
    blocks = x_ref.shape[0] // BS
    half = blocks // 2
    zh = nz // 2
    rows = ROWS
    per_dest = rows * chunks
    perms = perm_ref.shape[0]
    regs = con_ref.shape[0]
    nuis = nui_ref.shape[0]
    cdim = perms * regs

    fix, y = lax.axis_index("fix"), lax.axis_index("subj")
    q = lax.rem(fix, NQ)
    x = lax.rem(fix // NQ, NX)
    z = fix // (NQ * NX)
    m = x * NQ + q

    def fix_of(zz, xx, qq):
        return (zz * NX + xx) * NQ + qq

    x_by = {0: x, 1: x + 1 - 2 * lax.rem(x, 2), 2: lax.rem(x + 2, NX), 3: NX - 1 - x}
    q_by = {0: q, 1: 1 - q}
    y_to = [lax.rem(y + 1, ny), lax.rem(y + ny - 1, ny)]
    z_to = [lax.rem(z + 1, nz), lax.rem(z + nz - 1, nz)]

    def y_dev(d):
        return (fix, y_to[d])

    def z_dev(d):
        return (fix_of(z_to[d], x, q), y)

    def x_dev(o):
        return (fix_of(z, x_by[o // 2], q_by[o % 2]), y)

    def x_slot(o):
        return x_by[o // 2] * NQ + q_by[o % 2]

    peers = [y_dev(0), y_dev(1), z_dev(0), z_dev(1)] + [x_dev(o) for o in range(1, 8)]
    barrier = pltpu.get_barrier_semaphore()
    for peer in peers:
        pl.semaphore_signal(barrier, inc=1, device_id=peer, device_id_type=MESH)

    tile_copy = pltpu.make_async_copy(t_ref, tv, loc.at[0])
    tile_copy.start()
    sent = []

    def remote(src, dst, send_sem, recv_sem, device):
        copy = pltpu.make_async_remote_copy(
            src_ref=src, dst_ref=dst, send_sem=send_sem, recv_sem=recv_sem,
            device_id=device, device_id_type=MESH,
        )
        copy.start()
        sent.append(copy)
        return copy

    index = perm_ref[...]
    group, lane = index // BS, lax.rem(index, BS)
    for r in range(regs):
        picked = jnp.zeros((perms, BS), F32)
        for g in range(con_ref.shape[1] // BS):
            table = jnp.broadcast_to(con_ref[r : r + 1, g * BS : (g + 1) * BS], (perms, BS))
            value = jnp.take_along_axis(table, lane, axis=1, mode="promise_in_bounds")
            picked = jnp.where(group == g, value, picked)
        dsc[pl.ds(r, perms, stride=regs), :] = picked
    for i, piece in enumerate(split3(dsc[...], True)):
        dcat[0:cdim, i * BS : (i + 1) * BS] = piece
    pinv = jnp.concatenate([pinv_ref[...], jnp.zeros((16 - nuis, BS), F32)], axis=0)
    for i, piece in enumerate(split3(pinv, True)):
        dcat[cdim : cdim + 16, i * BS : (i + 1) * BS] = piece
    for i, piece in enumerate(split3(x_ref[...], False)):
        xcat[:, i * BS : (i + 1) * BS] = piece
    nui = jnp.concatenate([jnp.zeros((nuis, BS), F32), nui_ref[...], jnp.zeros((16 - 2 * nuis, BS), F32)], axis=0)
    ncat = jnp.concatenate(split3(nui, False), axis=1)
    load = lax.dot_general(ncat, dcat[0:cdim, :], NT, preferred_element_type=F32)
    for i in range(cdim // BS):
        mts[i] = load[0:EXTRA, i * BS : (i + 1) * BS]
    for b in range(0, blocks, 2):
        both = lax.dot_general(dcat[...], xcat[b * BS : (b + 2) * BS, :], NT, preferred_element_type=F32)
        for i in range(2):
            mine = both[:, i * BS : (i + 1) * BS]
            part[:, b + i] = mine[0:cdim].reshape(ny, per_dest, BS)
            gpart[b + i] = mine[cdim : cdim + EXTRA]

    def store_own(ref, dest, c, lo, hi, add):
        top = part[dest, lo:hi, c * rows : (c + 1) * rows, :]
        ref[lo:hi, 0:rows, :] = ref[lo:hi, 0:rows, :] + top if add else top
        if c == 0:
            more = gpart[lo:hi]
            ref[lo:hi, rows : rows + EXTRA, :] = ref[lo:hi, rows : rows + EXTRA, :] + more if add else more
            if lo == 0:
                per = BS // per_dest
                ref[0, rows : rows + EXTRA, :] = ref[0, rows : rows + EXTRA, :] + mts[dest // per]

    pl.semaphore_wait(barrier, len(peers))

    rq[m] = req_ref[...]
    asks = [remote(req_ref, rq.at[m], qs.at[o], qv.at[o], x_dev(o)) for o in range(1, 8)]
    flights = {}

    def step_s0(c, _):
        store_own(sb[c], lax.rem(y + hy, ny), c, 0, blocks, False)
        flights["y", c, 0, 0] = remote(
            sb[c].at[0:half], rb[c].at[0, 0, 0:half], ys.at[c, 0, 0], yr.at[c, 0, 0], y_dev(0))
        flights["y", c, 0, 1] = remote(
            sb[c].at[half:blocks], rb[c].at[1, 0, half:blocks], ys.at[c, 0, 1], yr.at[c, 0, 1], y_dev(1))

    def step_a(c, s):
        for d in range(2):
            flights["y", c, s, d].wait_recv()
            far = hy - 1 - s
            dest = lax.rem(y + (far if d == 0 else ny - far), ny)
            held = rb[c].at[d, s]
            if s == 0:
                lo, hi = (0, half) if d == 0 else (half, blocks)
                store_own(held, dest, c, lo, hi, True)
                other = (half, blocks) if d == 0 else (0, half)
                store_own(held, dest, c, other[0], other[1], False)
            else:
                store_own(held, dest, c, 0, blocks, True)
            flights["y", c, s + 1, d] = remote(
                held, rb[c].at[d, s + 1], ys.at[c, s + 1, d], yr.at[c, s + 1, d], y_dev(d))

    def z_send(c, s, d):
        src = lax.rem(z + (nz - s if d == 0 else s), nz)
        ref = zb[c].at[src]
        if s == hz - 1:
            ref = zb[c].at[src, 0:half] if d == 0 else zb[c].at[src, half:blocks]
        flights["z", c, s, d] = remote(ref, ref, zs.at[c, s, d], zr.at[c, s, d], z_dev(d))

    def step_fin(c, _):
        for d in range(2):
            flights["y", c, hy - 1, d].wait_recv()
        held = rb[c].at[0, hy - 1]
        store_own(held, y, c, 0, blocks, True)
        if c == 0:
            more = held[:, rows : rows + EXTRA, :] + rb[c][1, hy - 1, :, rows : rows + EXTRA, :]
            gfin[...] = more
            square = jnp.concatenate([more[0], jnp.zeros((BS - EXTRA, BS), F32)], axis=0)
            mcol[...] = jnp.transpose(square)
        total = held[:, 0:rows, :] + rb[c][1, hy - 1, :, 0:rows, :]
        per = BS // per_dest
        cols = mcol[pl.ds(lax.rem(y, per) * per_dest + c * rows, rows), :]
        for n in range(nuis):
            weight = jnp.broadcast_to(cols[:, nuis + n : nuis + n + 1], (rows, BS))
            total = total - weight[None] * gfin[:, n : n + 1, :]
        zb[c][z] = total
        for d in range(2):
            z_send(c, 0, d)

    def step_zf(c, s):
        for d in range(2):
            flights["z", c, s, d].wait_recv()
            z_send(c, s + 1, d)

    ready_asks = []

    def step_xp(c, _):
        if not ready_asks:
            for ask in asks:
                ask.wait_recv()
            copy = pltpu.make_async_copy(rq, rqs, loc.at[1])
            copy.start()
            copy.wait()
            ready_asks.append(1)
        for d in range(2):
            flights["z", c, hz - 1, d].wait_recv()
        for o in (4, 5) + DIRECT:
            e = x_slot(o)
            for zz in range(nz):
                pk[c][o, zz] = zb[c][zz, rqs[e, zz, m]]
            if o in (4, 5):
                for way in range(2):
                    flights["h", c, way, o - 4] = remote(
                        pk[c].at[o, way * zh : (way + 1) * zh], rl[c].at[way, o - 4],
                        hs.at[c, way, o - 4], hv.at[c, way, o - 4], x_dev(2 if way == 0 else 6))
            else:
                flights["x", c, o] = remote(pk[c].at[o], xr[c].at[m], xs.at[c, o], xv.at[c, o], x_dev(o))
        for zz in range(nz):
            xr[c][m, zz] = zb[c][zz, rqs[m, zz, m]]

    def step_xf(c, _):
        for way in range(2):
            for b in range(2):
                flights["h", c, way, b].wait_recv()
                source = x_slot(2 if way == 0 else 6)
                flights["f", c, way, b] = remote(
                    rl[c].at[way, b], xr[c].at[source, way * zh : (way + 1) * zh],
                    fs.at[c, way, b], fv.at[c, way, b], x_dev((6 if way == 0 else 2) + b))

    def step_tp(b, _):
        if b == 0:
            tile_copy.wait()
        for k in range(tv.shape[1]):
            tile = tv[b, k]
            high = tile.astype(BF16)
            thi[b, :, k * BS : (k + 1) * BS] = high
            tlo[b, :, k * BS : (k + 1) * BS] = (tile - high.astype(F32)).astype(BF16)

    def step_sm(c, _):
        for o in DIRECT:
            flights["x", c, o].wait_recv()
        for way in range(2):
            for b in range(2):
                flights["f", c, way, b].wait_recv()
        for b in range(blocks):
            pieces = []
            for k in range(tv.shape[1]):
                col = col_ref[b, k]
                owner = col // blocks
                pieces.append(xr[c][lax.rem(owner, NX * NQ), owner // (NX * NQ)])
            value = jnp.concatenate(pieces, axis=1)
            high = value.astype(BF16).astype(F32)
            both = jnp.concatenate([high, value - high], axis=0).astype(BF16)
            first = lax.dot_general(both, thi[b], NT, preferred_element_type=F32)
            second = lax.dot_general(both, tlo[b], NT, preferred_element_type=F32)
            out_ref[c * rows : (c + 1) * rows, b * BS : (b + 1) * BS] = (
                first[0:rows] + (first[rows:] + second[0:rows]))

    steps = dict(s0=step_s0, a=step_a, fin=step_fin, zf=step_zf, xp=step_xp, xf=step_xf, tp=step_tp, sm=step_sm)
    for name, which, step in plan(chunks, hy, hz, blocks, rows):
        steps[name](which, step)
    for copy in sent:
        copy.wait_send()


def per_device(fixels, conn_tiles, columns, nuisance, nuisance_pinv, contrast, perm_table):
    ny = lax.axis_size("subj")
    nz = lax.axis_size("fix") // (NX * NQ)
    blocks, tiles = columns.shape
    fixel_count = fixels.shape[0]
    perms, regs = perm_table.shape[0], contrast.shape[0]
    cdim = perms * regs
    per_dest = cdim // ny
    chunks = per_dest // ROWS
    wanted = columns.reshape(1, 1, -1)
    group = NX * NQ
    line = lax.broadcasted_iota(jnp.int32, (nz, BS, 1), 0)
    lane = lax.broadcasted_iota(jnp.int32, (nz, BS, 1), 1)
    hit = jnp.logical_and(wanted // blocks == line * group + lane, lane < group)
    request = jnp.sum(jnp.where(hit, wanted % blocks, 0), axis=2)
    vm = pltpu.VMEM
    rc = [ROWS + (EXTRA if c == 0 else 0) for c in range(chunks)]
    hy, hz = ny // 2, nz // 2
    sem = pltpu.SemaphoreType.DMA
    scratch = [
        vm((cdim, BS), F32), vm((cdim + 16, 3 * BS), BF16), vm((fixel_count, 3 * BS), BF16),
        vm((ny, blocks, per_dest, BS), F32), vm((blocks, EXTRA, BS), F32), vm((cdim // BS, EXTRA, BS), F32),
        vm((blocks, EXTRA, BS), F32), vm((BS, BS), F32),
        vm(conn_tiles.shape, F32), vm((blocks, BS, tiles * BS), BF16), vm((blocks, BS, tiles * BS), BF16),
        vm((group, nz, BS), jnp.int32), pltpu.SMEM((group, nz, BS), jnp.int32),
    ]
    scratch += [vm((blocks, r, BS), F32) for r in rc]
    scratch += [vm((2, hy, blocks, r, BS), F32) for r in rc]
    scratch += [vm((nz, blocks, ROWS, BS), F32) for _ in rc]
    scratch += [vm((group, nz, ROWS, BS), F32) for _ in rc]
    scratch += [vm((group, nz, ROWS, BS), F32) for _ in rc]
    scratch += [vm((2, 2, nz // 2, ROWS, BS), F32) for _ in rc]
    scratch += [
        sem((chunks, hy, 2)), sem((chunks, hy, 2)), sem((chunks, hz, 2)), sem((chunks, hz, 2)),
        sem((chunks, 8)), sem((chunks, 8)), sem((chunks, 2, 2)), sem((chunks, 2, 2)),
        sem((chunks, 2, 2)), sem((chunks, 2, 2)), sem((8,)), sem((8,)), sem((2,)),
    ]
    spec = pl.BlockSpec(memory_space=pltpu.VMEM)
    return pl.pallas_call(
        functools.partial(kernel, ny, nz, chunks),
        out_shape=jax.ShapeDtypeStruct((per_dest, fixel_count), F32),
        in_specs=[spec, pl.BlockSpec(memory_space=pl.ANY), spec, spec, spec, spec, spec,
                  pl.BlockSpec(memory_space=pltpu.SMEM)],
        out_specs=spec,
        scratch_shapes=scratch,
        compiler_params=pltpu.CompilerParams(collective_id=0, has_side_effects=True),
        name="project_exchange",
    )(fixels, conn_tiles, perm_table, contrast, nuisance, nuisance_pinv, request, columns)


def solution(mesh):
    placed = (
        P("fix", "subj"),
        P("fix", None, None, None),
        P("fix", None),
        P(None, "subj"),
        P(None, "subj"),
        P(),
        P(None, "subj"),
    )
    return jax.shard_map(
        per_device, mesh=mesh, in_specs=placed, out_specs=P("subj", "fix"), check_vma=False
    )
```

time: 233 us -> 84.9 us (0.36); the launches traced: 229 us -> 84.7 us
  Pallas kernels: 0 us -> 81.4 us
  waiting for transfers between devices: 76.8 us -> 0 us
  local copies, waits for them, and re-layouts: 70.1 us -> 2.51 us
  blocking collectives: 47.3 us -> 0 us
  between operations: 13.5 us -> 0.01 us
  matrix products: 8.82 us -> 0 us
  starting transfers between devices: 5.88 us -> 0 us
  other arithmetic: 6.09 us -> 0.79 us
    pallas_call x0 -> x1, Pallas kernels: none -> 81.4 us  [per_device(): pl.pallas_call(functools.partial(kernel, ny, nz, chunks), out_shape=jax.S...]
    gather x4 -> x0, local copies, waits for them, and re-layouts: 67.9 us -> none  [the longest x2 59.9 us: design_rows(): picked = jnp.take(contrast, perm_table, axis=1)]
    reduce_scatter x1 -> x0, waiting for transfers between devices: 42.4 us -> none  [per_device(): lax.psum_scatter(partial_value, 'subj', scatter_dimension=0, tiled=True)]
    all_to_all x1 -> x0, waiting for transfers between devices: 34.4 us -> none  [per_device(): lax.all_to_all(outgoing, 'fix', split_axis=0, concat_axis=0, tiled=True)]
    all_to_all x1 -> x0, blocking collectives: 24 us -> none  [per_device(): lax.all_to_all(request.reshape(fix_count, capacity), 'fix', split_axis=0,...]
    psum x1 -> x0, blocking collectives: 23.3 us -> none  [per_device(): fitted = lax.psum(fitted_part, 'subj')]
    dot_general x4 -> x0, matrix products: 8.82 us -> none  [the longest x1 4.12 us: per_device(): jnp.einsum('bkij,bkjs->bis', conn_tiles, needed, precision=lax.Precision....]
    all_to_all x1 -> x0, starting transfers between devices: 5.84 us -> none  [per_device(): lax.all_to_all(outgoing, 'fix', split_axis=0, concat_axis=0, tiled=True)]
  transfers between devices with their start and end apart: 2 -> 0, of which waited for: 2 -> 0; matrix products, arithmetic and copies ran while one was open for 26% -> 0% of each run, Pallas kernels for 0% -> 0%
where the time goes in v2:
time: 84.9 us; the launch traced here: 84.7 us
  Pallas kernels  81.4 us (96%)
  local copies, waits for them, and re-layouts  2.51 us (3%)
    pallas_call x1, Pallas kernels, per_device(): pl.pallas_call(functools.partial(kernel, ny, nz, chunks), out_shape=jax.S...  81.4 us
    unnamed x4, local copies, waits for them, and re-layouts  2.43 us

profile of v2, /device:TPU:1, one launch (start us, length us, event | category | flops | bytes accessed | tf_op | source)
XLA Modules:
  0.0 84.7 jit_solution(14414071665461345009)
XLA Ops:
  0.0 0.1 iota_add_fusion
  0.1 0.8 copy.12.refs_7_
  0.8 0.0 copy-start
  0.8 0.1 reshape.110
  0.9 0.7 select_reduce_fusion.refs_6_
  1.6 0.0 copy-done
  1.6 81.4 %project_exchange.1 = f32[64,1024]{1,0:T(8,128)} custom-call(f32[1024,128]{1,0:T(8,128)} %refs_0_.1, f32[8,4,128,128]{3,2,1,0:T(8,128)} %refs_1_.1, s32[128,128]{1,0:T(8,128)} %refs_2_.1, f32[4,1024]{1,0:T(4,128)} %refs_3_.1, f32[4,128]{1,0:T(4,128)} %refs_4_.1, f32[4,128]{1,0:T(4,128)} %refs_5_.1, s32[8,128]{1,0:T(8,128)} %select_reduce_fusion.refs_6_, ...), custom_call_target="tpu_custom_call" | custom-call | tf_op jit(solution)/shard_map/project_exchange/pallas_call | solution.py:357
  83.0 1.7 %copy.15 = f32[64,1024]{1,0:T(8,128)} copy(f32[64,1024]{1,0:T(8,128)} %project_exchange.1) | data formatting | bytes 524288
  (3 shorter events, 0.0 us)
Async XLA Ops:
  0.8 0.8 copy-start

commit v3 on v2

v3 whole, which is shorter than its diff:
```python
import functools

import jax
import jax.numpy as jnp
from jax import lax
from jax.experimental import pallas as pl
from jax.experimental.pallas import tpu as pltpu
from jax.sharding import PartitionSpec as P

MESH = pl.DeviceIdType.MESH
F32, BF16 = jnp.float32, jnp.bfloat16
BS = 128
NX, NQ = 4, 2
ROWS = 8
WINDOW = 4
RATE, LATENCY = 50e3, 1.8
EXTRA = 8
NT = (((1,), (1,)), ((), ()))
PARTNERS = (4, 5, 2, 3, 6, 7, 1)


def plan(chunks, hy, hz, tiles, rows):
    rate, lat = RATE, LATENCY
    size = rows * BS * 4 * 8
    cost = dict(s0=0.1, a=0.2, fin=0.3, zf=0.05, xp=0.5, sm=1.2, tp=0.3)
    stages = [("s0", 0)] + [("a", s) for s in range(hy - 1)] + [("fin", 0)]
    stages += [("zf", s) for s in range(hz - 1)] + [("xp", 0), ("sm", 0)]
    free = dict(y=0.0, z=0.0, x=0.0)
    at, ready = [0] * chunks, [0.0] * chunks
    order, t, prepared = [], 0.0, 0

    def send(link, amount):
        free[link] = max(free[link], t) + amount / rate
        return free[link] + lat

    while any(i < len(stages) for i in at):
        best, late, soonest = None, None, 1e9
        for c in range(chunks):
            if at[c] == len(stages):
                continue
            when = ready[c]
            if at[c] == 0:
                if c and at[c - 1] == 0:
                    continue
                if sum(0 < i <= hy for i in at) >= WINDOW:
                    continue
                when = max(when, free["y"] - 0.3)
            if stages[at[c]][0] == "sm":
                if prepared < tiles:
                    continue
                if when <= t and late is None:
                    late = c
            elif when <= t and best is None:
                best = c
            soonest = min(soonest, when)
        best = late if best is None else best
        if best is None:
            if prepared < tiles and order:
                order.append(("tp", prepared, 0))
                prepared += 1
                t += cost["tp"]
            else:
                t = max(soonest, t + 1e-6)
            continue
        name, step = stages[at[best]]
        order.append((name, best, step))
        t += cost[name]
        if name == "s0":
            ready[best] = send("y", size / 2)
        elif name == "a":
            ready[best] = send("y", size)
        elif name == "fin":
            ready[best] = send("z", size)
        elif name == "zf":
            ready[best] = send("z", size if step < hz - 2 else size / 2)
        elif name == "xp":
            ready[best] = send("x", 4 * size) + 0.7
        at[best] += 1
    return order


def split3(value, first):
    high = value.astype(BF16)
    low = (value - high.astype(F32)).astype(BF16)
    return [high, high, low] if first else [high, low, high]


def kernel(ny, nz, chunks, *refs):
    (x_hbm, t_ref, perm_hbm, con_hbm, nui_hbm, pinv_hbm, col_hbm, out_ref), refs = refs[:8], refs[8:]
    (x_ref, perm_ref, con_ref, nui_ref, pinv_ref, req_ref, col_ref), refs = refs[:7], refs[7:]
    dsc, dcat, xcat, part, gpart, mts, gfin, mcol, tv, thi, tlo, rq, rqs = refs[:13]
    refs = refs[13:]
    sb, refs = refs[:chunks], refs[chunks:]
    rb, refs = refs[:chunks], refs[chunks:]
    zb, refs = refs[:chunks], refs[chunks:]
    pk, refs = refs[:chunks], refs[chunks:]
    xr, refs = refs[:chunks], refs[chunks:]
    ys, yr, zr, xv, one, loc = refs
    hy, hz = ny // 2, nz // 2
    blocks = x_ref.shape[0] // BS
    half = blocks // 2
    rows = ROWS
    per_dest = rows * chunks
    perms = perm_ref.shape[0]
    regs = con_ref.shape[0]
    nuis = nui_ref.shape[0]
    cdim = perms * regs

    fix, y = lax.axis_index("fix"), lax.axis_index("subj")
    q = lax.rem(fix, NQ)
    x = lax.rem(fix // NQ, NX)
    z = fix // (NQ * NX)
    m = x * NQ + q

    def fix_of(zz, xx, qq):
        return (zz * NX + xx) * NQ + qq

    x_by = {0: x, 1: x + 1 - 2 * lax.rem(x, 2), 2: lax.rem(x + 2, NX), 3: NX - 1 - x}
    q_by = {0: q, 1: 1 - q}
    y_to = [lax.rem(y + 1, ny), lax.rem(y + ny - 1, ny)]
    z_to = [lax.rem(z + 1, nz), lax.rem(z + nz - 1, nz)]

    def y_dev(d):
        return (fix, y_to[d])

    def z_dev(d):
        return (fix_of(z_to[d], x, q), y)

    def x_dev(o):
        return (fix_of(z, x_by[o // 2], q_by[o % 2]), y)

    def x_slot(o):
        return x_by[o // 2] * NQ + q_by[o % 2]

    peers = [y_dev(0), y_dev(1), z_dev(0), z_dev(1)] + [x_dev(o) for o in range(1, 8)]
    barrier = pltpu.get_barrier_semaphore()
    for peer in peers:
        pl.semaphore_signal(barrier, inc=1, device_id=peer, device_id_type=MESH)

    loads = []
    for i, (src, dst) in enumerate((
        (perm_hbm, perm_ref), (con_hbm, con_ref), (x_hbm, x_ref), (nui_hbm, nui_ref),
        (pinv_hbm, pinv_ref), (col_hbm, col_ref), (t_ref, tv),
    )):
        loads.append(pltpu.make_async_copy(src, dst, loc.at[i]))
        loads[-1].start()

    def arrived(ref, sem):
        pltpu.make_async_copy(ref, ref, sem).wait()

    def remote(src, dst, send_sem, recv_sem, device):
        copy = pltpu.make_async_remote_copy(
            src_ref=src, dst_ref=dst, send_sem=send_sem, recv_sem=recv_sem,
            device_id=device, device_id_type=MESH,
        )
        copy.start()

    loads[0].wait()
    loads[1].wait()
    index = perm_ref[...]
    group, lane = index // BS, lax.rem(index, BS)
    for r in range(regs):
        picked = jnp.zeros((perms, BS), F32)
        for g in range(con_ref.shape[1] // BS):
            table = jnp.broadcast_to(con_ref[r : r + 1, g * BS : (g + 1) * BS], (perms, BS))
            value = jnp.take_along_axis(table, lane, axis=1, mode="promise_in_bounds")
            picked = jnp.where(group == g, value, picked)
        dsc[pl.ds(r, perms, stride=regs), :] = picked
    for i, piece in enumerate(split3(dsc[...], True)):
        dcat[0:cdim, i * BS : (i + 1) * BS] = piece
    for i in range(2, 6):
        loads[i].wait()
    pinv = jnp.concatenate([pinv_ref[...], jnp.zeros((16 - nuis, BS), F32)], axis=0)
    for i, piece in enumerate(split3(pinv, True)):
        dcat[cdim : cdim + 16, i * BS : (i + 1) * BS] = piece
    for i, piece in enumerate(split3(x_ref[...], False)):
        xcat[:, i * BS : (i + 1) * BS] = piece
    nui = jnp.concatenate([jnp.zeros((nuis, BS), F32), nui_ref[...], jnp.zeros((16 - 2 * nuis, BS), F32)], axis=0)
    ncat = jnp.concatenate(split3(nui, False), axis=1)
    load = lax.dot_general(ncat, dcat[0:cdim, :], NT, preferred_element_type=F32)
    for i in range(cdim // BS):
        mts[i] = load[0:EXTRA, i * BS : (i + 1) * BS]
    for b in range(0, blocks, 2):
        both = lax.dot_general(dcat[...], xcat[b * BS : (b + 2) * BS, :], NT, preferred_element_type=F32)
        for i in range(2):
            mine = both[:, i * BS : (i + 1) * BS]
            part[:, b + i] = mine[0:cdim].reshape(ny, per_dest, BS)
            gpart[b + i] = mine[cdim : cdim + EXTRA]

    def store_own(ref, dest, c, lo, hi, add):
        top = part[dest, lo:hi, c * rows : (c + 1) * rows, :]
        ref[lo:hi, 0:rows, :] = ref[lo:hi, 0:rows, :] + top if add else top
        if c == 0:
            more = gpart[lo:hi]
            ref[lo:hi, rows : rows + EXTRA, :] = ref[lo:hi, rows : rows + EXTRA, :] + more if add else more
            if lo == 0:
                per = BS // per_dest
                ref[0, rows : rows + EXTRA, :] = ref[0, rows : rows + EXTRA, :] + mts[dest // per]

    line = lax.broadcasted_iota(jnp.int32, (nz, BS), 0)
    place = lax.broadcasted_iota(jnp.int32, (nz, BS), 1)
    place = jnp.where(place < NX * NQ, line * (NX * NQ) + place, -1)
    request = jnp.zeros((nz, BS), jnp.int32)
    for b in range(blocks):
        for k in range(tv.shape[1]):
            col = col_ref[k, b]
            request = jnp.where(place == col // blocks, lax.rem(col, blocks), request)
    req_ref[...] = request
    rq[m] = request

    pl.semaphore_wait(barrier, len(peers))

    def step_s0(c, _):
        store_own(sb[c], lax.rem(y + hy, ny), c, 0, blocks, False)
        out = ys.at[min(c, 1)]
        remote(sb[c].at[0:half], rb[c].at[0, 0:half], out, yr.at[c, 0], y_dev(0))
        remote(sb[c].at[half:blocks], rb[c].at[1, half:blocks], out, yr.at[c, 0], y_dev(1))
        if c == 0:
            for o in range(1, 8):
                remote(req_ref, rq.at[m], one.at[2], one.at[3], x_dev(o))

    def step_a(c, s):
        arrived(rb[c].at[0] if s == 0 else rb[c].at[0:2], yr.at[c, s % 2])
        for d in range(2):
            far = hy - 1 - s
            dest = lax.rem(y + (far if d == 0 else ny - far), ny)
            held = rb[c].at[2 * s + d]
            if s == 0:
                lo, hi = (0, half) if d == 0 else (half, blocks)
                store_own(held, dest, c, lo, hi, True)
                other = (half, blocks) if d == 0 else (0, half)
                store_own(held, dest, c, other[0], other[1], False)
            else:
                store_own(held, dest, c, 0, blocks, True)
            remote(held, rb[c].at[2 * s + 2 + d], ys.at[min(c, 1)], yr.at[c, (s + 1) % 2], y_dev(d))

    def z_send(c, s, d):
        src = lax.rem(z + (nz - s if d == 0 else s), nz)
        ref = zb[c].at[src]
        if s == hz - 1:
            ref = zb[c].at[src, 0:half] if d == 0 else zb[c].at[src, half:blocks]
        remote(ref, ref, one.at[0], zr.at[c, s % 2], z_dev(d))

    def step_fin(c, _):
        arrived(rb[c].at[0:2], yr.at[c, (hy - 1) % 2])
        held = rb[c].at[2 * hy - 2]
        store_own(held, y, c, 0, blocks, True)
        if c == 0:
            more = held[:, rows : rows + EXTRA, :] + rb[c][2 * hy - 1, :, rows : rows + EXTRA, :]
            gfin[...] = more
            square = jnp.concatenate([more[0], jnp.zeros((BS - EXTRA, BS), F32)], axis=0)
            mcol[...] = jnp.transpose(square)
        total = held[:, 0:rows, :] + rb[c][2 * hy - 1, :, 0:rows, :]
        per = BS // per_dest
        cols = mcol[pl.ds(lax.rem(y, per) * per_dest + c * rows, rows), :]
        for n in range(nuis):
            weight = jnp.broadcast_to(cols[:, nuis + n : nuis + n + 1], (rows, BS))
            total = total - weight[None] * gfin[:, n : n + 1, :]
        zb[c][z] = total
        for d in range(2):
            z_send(c, 0, d)

    def step_zf(c, s):
        arrived(zb[c].at[0:2], zr.at[c, s % 2])
        for d in range(2):
            z_send(c, s + 1, d)

    ready_asks = []

    def step_xp(c, _):
        if not ready_asks:
            arrived(rq.at[0:7], one.at[3])
            copy = pltpu.make_async_copy(rq, rqs, loc.at[7])
            copy.start()
            copy.wait()
            ready_asks.append(1)
        arrived(zb[c].at[0:1], zr.at[c, (hz - 1) % 2])
        for o in PARTNERS:
            e = x_slot(o)
            for zz in range(nz):
                pk[c][o, zz] = zb[c][zz, rqs[e, zz, m]]
            remote(pk[c].at[o], xr[c].at[m], one.at[1], xv.at[c], x_dev(o))
        for zz in range(nz):
            xr[c][m, zz] = zb[c][zz, rqs[m, zz, m]]

    def step_tp(b, _):
        if b == 0:
            loads[6].wait()
        for k in range(tv.shape[1]):
            tile = tv[b, k]
            high = tile.astype(BF16)
            thi[b, :, k * BS : (k + 1) * BS] = high
            tlo[b, :, k * BS : (k + 1) * BS] = (tile - high.astype(F32)).astype(BF16)

    def step_sm(c, _):
        arrived(xr[c].at[0:7], xv.at[c])
        for b in range(blocks):
            pieces = []
            for k in range(tv.shape[1]):
                col = col_ref[k, b]
                owner = col // blocks
                pieces.append(xr[c][lax.rem(owner, NX * NQ), owner // (NX * NQ)])
            value = jnp.concatenate(pieces, axis=1)
            high = value.astype(BF16).astype(F32)
            both = jnp.concatenate([high, value - high], axis=0).astype(BF16)
            first = lax.dot_general(both, thi[b], NT, preferred_element_type=F32)
            second = lax.dot_general(both, tlo[b], NT, preferred_element_type=F32)
            out_ref[c * rows : (c + 1) * rows, b * BS : (b + 1) * BS] = (
                first[0:rows] + (first[rows:] + second[0:rows]))

    steps = dict(s0=step_s0, a=step_a, fin=step_fin, zf=step_zf, xp=step_xp, tp=step_tp, sm=step_sm)
    for name, which, step in plan(chunks, hy, hz, blocks, rows):
        steps[name](which, step)
    arrived(rb[0].at[0 : 2 * hy - 1], ys.at[0])
    arrived(part.at[0 : 2 * hy - 1, :, rows:per_dest], ys.at[1])
    arrived(part.at[0 : 2 * hz - 1], one.at[0])
    arrived(part.at[0:7], one.at[1])
    arrived(rq.at[0:7], one.at[2])


def per_device(fixels, conn_tiles, columns, nuisance, nuisance_pinv, contrast, perm_table):
    ny = lax.axis_size("subj")
    nz = lax.axis_size("fix") // (NX * NQ)
    blocks, tiles = columns.shape
    fixel_count = fixels.shape[0]
    perms, regs = perm_table.shape[0], contrast.shape[0]
    cdim = perms * regs
    per_dest = cdim // ny
    chunks = per_dest // ROWS
    group = NX * NQ
    vm = pltpu.VMEM
    rc = [ROWS + (EXTRA if c == 0 else 0) for c in range(chunks)]
    hy, hz = ny // 2, nz // 2
    sem = pltpu.SemaphoreType.DMA
    scratch = [
        vm(fixels.shape, F32), vm(perm_table.shape, jnp.int32), vm(contrast.shape, F32), vm(nuisance.shape, F32),
        vm(nuisance_pinv.shape, F32), vm((nz, BS), jnp.int32), pltpu.SMEM((tiles, blocks), jnp.int32),
        vm((cdim, BS), F32), vm((cdim + 16, 3 * BS), BF16), vm((fixel_count, 3 * BS), BF16),
        vm((ny, blocks, per_dest, BS), F32), vm((blocks, EXTRA, BS), F32), vm((cdim // BS, EXTRA, BS), F32),
        vm((blocks, EXTRA, BS), F32), vm((BS, BS), F32),
        vm(conn_tiles.shape, F32), vm((blocks, BS, tiles * BS), BF16), vm((blocks, BS, tiles * BS), BF16),
        vm((group, nz, BS), jnp.int32), pltpu.SMEM((group, nz, BS), jnp.int32),
    ]
    scratch += [vm((blocks, r, BS), F32) for r in rc]
    scratch += [vm((2 * hy, blocks, r, BS), F32) for r in rc]
    scratch += [vm((nz, blocks, ROWS, BS), F32) for _ in rc]
    scratch += [vm((group, nz, ROWS, BS), F32) for _ in rc]
    scratch += [vm((group, nz, ROWS, BS), F32) for _ in rc]
    scratch += [
        sem((2,)), sem((chunks, 2)), sem((chunks, 2)), sem((chunks,)), sem((4,)), sem((8,)),
    ]
    return pl.pallas_call(
        functools.partial(kernel, ny, nz, chunks),
        out_shape=jax.ShapeDtypeStruct((per_dest, fixel_count), F32),
        in_specs=[pl.BlockSpec(memory_space=pl.ANY)] * 7,
        out_specs=pl.BlockSpec(memory_space=pltpu.VMEM),
        scratch_shapes=scratch,
        compiler_params=pltpu.CompilerParams(collective_id=0, has_side_effects=True),
        name="project_exchange",
    )(fixels, conn_tiles, perm_table, contrast, nuisance, nuisance_pinv, columns.T)


def solution(mesh):
    placed = (
        P("fix", "subj"),
        P("fix", None, None, None),
        P("fix", None),
        P(None, "subj"),
        P(None, "subj"),
        P(),
        P(None, "subj"),
    )
    return jax.shard_map(
        per_device, mesh=mesh, in_specs=placed, out_specs=P("subj", "fix"), check_vma=False
    )
```

time: 84.9 us -> 73.8 us (0.87)
  Pallas kernels: 81.4 us -> 72 us
    pallas_call x1, Pallas kernels: 81.4 us -> 72 us  [per_device(): pl.pallas_call(functools.partial(kernel, ny, nz, chunks), out_shape=jax.S...]
    unnamed x4 -> x1, local copies, waits for them, and re-layouts: 2.43 us -> 1.67 us
where the time goes in v3:
time: 73.8 us; the launch traced here: 73.7 us
  Pallas kernels  72 us (98%)
  local copies, waits for them, and re-layouts  1.67 us (2%)
    pallas_call x1, Pallas kernels, per_device(): pl.pallas_call(functools.partial(kernel, ny, nz, chunks), out_shape=jax.S...  72 us
    unnamed x1, local copies, waits for them, and re-layouts  1.67 us

profile of v3, /device:TPU:1, one launch (start us, length us, event | category | flops | bytes accessed | tf_op | source)
XLA Modules:
  0.0 73.7 jit_solution(16117557845468245522)
XLA Ops:
  0.0 72.0 %project_exchange.1 = f32[64,1024]{1,0:T(8,128)} custom-call(f32[1024,128]{1,0:T(8,128)} %refs_0_.1, f32[8,4,128,128]{3,2,1,0:T(8,128)} %refs_1_.1, s32[128,128]{1,0:T(8,128)} %refs_2_.1, f32[4,1024]{1,0:T(4,128)} %refs_3_.1, f32[4,128]{1,0:T(4,128)} %refs_4_.1, f32[4,128]{1,0:T(4,128)} %refs_5_.1, s32[4,8]{1,0:T(4,128)} %bitcast.1), custom_call_target="tpu_custom_call" | custom-call | tf_op jit(solution)/shard_map/project_exchange/pallas_call | solution.py:352
  72.0 1.7 %copy.9 = f32[64,1024]{1,0:T(8,128)} copy(f32[64,1024]{1,0:T(8,128)} %project_exchange.1) | data formatting | bytes 524288

commit v4 on v3

--- a/solution.py
+++ b/solution.py
@@ -11,41 +11,42 @@
 F32, BF16 = jnp.float32, jnp.bfloat16
 BS = 128
 NX, NQ = 4, 2
-ROWS = 8
+ROWS = 16
 WINDOW = 4
-RATE, LATENCY = 50e3, 1.8
+RATE, LATENCY, GAP, SLACK = 50e3, 2.9, 0.1, 0.8
+SPANS = {0: (0, 1), 1: (1, 3), 2: (3, 5), 3: (5, 7), 4: (7, 8)}
 EXTRA = 8
 NT = (((1,), (1,)), ((), ()))
 PARTNERS = (4, 5, 2, 3, 6, 7, 1)
 
 
 def plan(chunks, hy, hz, tiles, rows):
-    rate, lat = RATE, LATENCY
     size = rows * BS * 4 * 8
-    cost = dict(s0=0.1, a=0.2, fin=0.3, zf=0.05, xp=0.5, sm=1.2, tp=0.3)
+    cost = dict(s0=0.1, a=0.1, fin=0.3, zf=0.2, xp=0.1, sm=0.8, tp=0.25)
     stages = [("s0", 0)] + [("a", s) for s in range(hy - 1)] + [("fin", 0)]
     stages += [("zf", s) for s in range(hz - 1)] + [("xp", 0), ("sm", 0)]
+    wire = dict(s0="y", a="y", fin="z", zf="z")
     free = dict(y=0.0, z=0.0, x=0.0)
     at, ready = [0] * chunks, [0.0] * chunks
     order, t, prepared = [], 0.0, 0
 
     def send(link, amount):
-        free[link] = max(free[link], t) + amount / rate
-        return free[link] + lat
+        free[link] = max(free[link], t) + amount / RATE + GAP
+        return free[link] + LATENCY
 
     while any(i < len(stages) for i in at):
         best, late, soonest = None, None, 1e9
         for c in range(chunks):
             if at[c] == len(stages):
                 continue
-            when = ready[c]
-            if at[c] == 0:
-                if c and at[c - 1] == 0:
-                    continue
-                if sum(0 < i <= hy for i in at) >= WINDOW:
-                    continue
-                when = max(when, free["y"] - 0.3)
-            if stages[at[c]][0] == "sm":
+            name, when = stages[at[c]][0], ready[c]
+            if name == "s0" and c and at[c - 1] == 0:
+                continue
+            if name == "s0" and sum(0 < i <= hy for i in at) >= WINDOW:
+                continue
+            if name in wire:
+                when = max(when, free[wire[name]] - SLACK)
+            if name == "sm":
                 if prepared < tiles:
                     continue
                 if when <= t and late is None:
@@ -73,8 +74,11 @@
             ready[best] = send("z", size)
         elif name == "zf":
             ready[best] = send("z", size if step < hz - 2 else size / 2)
-        elif name == "xp":
-            ready[best] = send("x", 4 * size) + 0.7
+        span = SPANS.get({"fin": 0, "zf": step + 1, "xp": hz}.get(name))
+        if span:
+            last = send("x", (span[1] - span[0]) * size / 2)
+            if name == "xp":
+                ready[best] = last + 0.7
         at[best] += 1
     return order
 
@@ -92,7 +96,7 @@
     refs = refs[13:]
     sb, refs = refs[:chunks], refs[chunks:]
     rb, refs = refs[:chunks], refs[chunks:]
-    zb, refs = refs[:chunks], refs[chunks:]
+    zb, refs = [refs[c * nz : (c + 1) * nz] for c in range(chunks)], refs[chunks * nz :]
     pk, refs = refs[:chunks], refs[chunks:]
     xr, refs = refs[:chunks], refs[chunks:]
     ys, yr, zr, xv, one, loc = refs
@@ -235,11 +239,37 @@
             remote(held, rb[c].at[2 * s + 2 + d], ys.at[min(c, 1)], yr.at[c, (s + 1) % 2], y_dev(d))
 
     def z_send(c, s, d):
-        src = lax.rem(z + (nz - s if d == 0 else s), nz)
-        ref = zb[c].at[src]
+        mine, theirs = ((nz - s) % nz, (nz - s - 1) % nz) if d == 0 else (s, s + 1)
+        src, dst = zb[c][mine], zb[c][theirs]
         if s == hz - 1:
-            ref = zb[c].at[src, 0:half] if d == 0 else zb[c].at[src, half:blocks]
-        remote(ref, ref, one.at[0], zr.at[c, s % 2], z_dev(d))
+            lo, hi = (0, half) if d == 0 else (half, blocks)
+            src, dst = src.at[lo:hi], dst.at[lo:hi]
+        remote(src, dst, one.at[0], zr.at[c, s % 2], z_dev(d))
+
+    slots = [0]
+    for far in range(1, hz):
+        slots += [far, nz - far]
+    slots.append(hz)
+    z_of = [lax.rem(z + slots[i], nz) for i in range(nz)]
+    ready_asks = []
+
+    def x_send(c, stage):
+        if not ready_asks:
+            arrived(rq.at[0:7], one.at[3])
+            copy = pltpu.make_async_copy(rq, rqs, loc.at[7])
+            copy.start()
+            copy.wait()
+            ready_asks.append(1)
+        if stage not in SPANS:
+            return
+        lo, hi = SPANS[stage]
+        for o in PARTNERS:
+            e = x_slot(o)
+            for i in range(lo, hi):
+                pk[c][o, i] = zb[c][slots[i]][rqs[e, z_of[i], m]]
+            remote(pk[c].at[o, lo:hi], xr[c].at[m, lo:hi], one.at[1], xv.at[c], x_dev(o))
+        for i in range(lo, hi):
+            xr[c][m, i] = zb[c][slots[i]][rqs[m, z_of[i], m]]
 
     def step_fin(c, _):
         arrived(rb[c].at[0:2], yr.at[c, (hy - 1) % 2])
@@ -256,32 +286,20 @@
         for n in range(nuis):
             weight = jnp.broadcast_to(cols[:, nuis + n : nuis + n + 1], (rows, BS))
             total = total - weight[None] * gfin[:, n : n + 1, :]
-        zb[c][z] = total
+        zb[c][0][...] = total
         for d in range(2):
             z_send(c, 0, d)
+        x_send(c, 0)
 
     def step_zf(c, s):
-        arrived(zb[c].at[0:2], zr.at[c, s % 2])
+        arrived(part.at[0:2, :, 0:rows], zr.at[c, s % 2])
         for d in range(2):
             z_send(c, s + 1, d)
-
-    ready_asks = []
+        x_send(c, s + 1)
 
     def step_xp(c, _):
-        if not ready_asks:
-            arrived(rq.at[0:7], one.at[3])
-            copy = pltpu.make_async_copy(rq, rqs, loc.at[7])
-            copy.start()
-            copy.wait()
-            ready_asks.append(1)
-        arrived(zb[c].at[0:1], zr.at[c, (hz - 1) % 2])
-        for o in PARTNERS:
-            e = x_slot(o)
-            for zz in range(nz):
-                pk[c][o, zz] = zb[c][zz, rqs[e, zz, m]]
-            remote(pk[c].at[o], xr[c].at[m], one.at[1], xv.at[c], x_dev(o))
-        for zz in range(nz):
-            xr[c][m, zz] = zb[c][zz, rqs[m, zz, m]]
+        arrived(part.at[0:1, :, 0:rows], zr.at[c, (hz - 1) % 2])
+        x_send(c, hz)
 
     def step_tp(b, _):
         if b == 0:
@@ -292,14 +310,25 @@
             thi[b, :, k * BS : (k + 1) * BS] = high
             tlo[b, :, k * BS : (k + 1) * BS] = (tile - high.astype(F32)).astype(BF16)
 
+    found = []
+
+    def find():
+        for b in range(blocks):
+            for k in range(tv.shape[1]):
+                owner = col_ref[k, b] // blocks
+                far = lax.rem(owner // (NX * NQ) + nz - z, nz)
+                slot = jnp.where(far < hz, jnp.maximum(2 * far - 1, 0), jnp.where(far == hz, nz - 1, 2 * (nz - far)))
+                found.append((lax.rem(owner, NX * NQ), slot))
+
     def step_sm(c, _):
+        if not found:
+            find()
         arrived(xr[c].at[0:7], xv.at[c])
         for b in range(blocks):
             pieces = []
             for k in range(tv.shape[1]):
-                col = col_ref[k, b]
-                owner = col // blocks
-                pieces.append(xr[c][lax.rem(owner, NX * NQ), owner // (NX * NQ)])
+                who, slot = found[b * tv.shape[1] + k]
+                pieces.append(xr[c][who, slot])
             value = jnp.concatenate(pieces, axis=1)
             high = value.astype(BF16).astype(F32)
             both = jnp.concatenate([high, value - high], axis=0).astype(BF16)
@@ -343,7 +372,7 @@
     ]
     scratch += [vm((blocks, r, BS), F32) for r in rc]
     scratch += [vm((2 * hy, blocks, r, BS), F32) for r in rc]
-    scratch += [vm((nz, blocks, ROWS, BS), F32) for _ in rc]
+    scratch += [vm((blocks, ROWS, BS), F32) for _ in rc for _ in range(nz)]
     scratch += [vm((group, nz, ROWS, BS), F32) for _ in rc]
     scratch += [vm((group, nz, ROWS, BS), F32) for _ in rc]
     scratch += [

time: 73.8 us -> 67.5 us (0.915)
  Pallas kernels: 72 us -> 65.7 us
    pallas_call x1, Pallas kernels: 72 us -> 65.7 us  [per_device(): pl.pallas_call(functools.partial(kernel, ny, nz, chunks), out_shape=jax.S...]
where the time goes in v4:
time: 67.5 us; the launch traced here: 67.4 us
  Pallas kernels  65.7 us (97%)
  local copies, waits for them, and re-layouts  1.67 us (2%)
    pallas_call x1, Pallas kernels, per_device(): pl.pallas_call(functools.partial(kernel, ny, nz, chunks), out_shape=jax.S...  65.7 us
    unnamed x1, local copies, waits for them, and re-layouts  1.67 us

profile of v4, /device:TPU:1, one launch (start us, length us, event | category | flops | bytes accessed | tf_op | source)
XLA Modules:
  0.0 67.4 jit_solution(9844395354217428743)
XLA Ops:
  0.0 65.7 %project_exchange.1 = f32[64,1024]{1,0:T(8,128)} custom-call(f32[1024,128]{1,0:T(8,128)} %refs_0_.1, f32[8,4,128,128]{3,2,1,0:T(8,128)} %refs_1_.1, s32[128,128]{1,0:T(8,128)} %refs_2_.1, f32[4,1024]{1,0:T(4,128)} %refs_3_.1, f32[4,128]{1,0:T(4,128)} %refs_4_.1, f32[4,128]{1,0:T(4,128)} %refs_5_.1, s32[4,8]{1,0:T(4,128)} %bitcast.1), custom_call_target="tpu_custom_call" | custom-call | tf_op jit(solution)/shard_map/project_exchange/pallas_call | solution.py:381
  65.7 1.7 %copy.9 = f32[64,1024]{1,0:T(8,128)} copy(f32[64,1024]{1,0:T(8,128)} %project_exchange.1) | data formatting | bytes 524288

commit v5 on v4

--- a/solution.py
+++ b/solution.py
@@ -92,14 +92,14 @@
 def kernel(ny, nz, chunks, *refs):
     (x_hbm, t_ref, perm_hbm, con_hbm, nui_hbm, pinv_hbm, col_hbm, out_ref), refs = refs[:8], refs[8:]
     (x_ref, perm_ref, con_ref, nui_ref, pinv_ref, req_ref, col_ref), refs = refs[:7], refs[7:]
-    dsc, dcat, xcat, part, gpart, mts, gfin, mcol, tv, thi, tlo, rq, rqs = refs[:13]
-    refs = refs[13:]
+    dsc, dcat, xcat, part, gpart, mts, gfin, mcol, tv, tcat, rq, rqs, eb, es = refs[:14]
+    refs = refs[14:]
     sb, refs = refs[:chunks], refs[chunks:]
     rb, refs = refs[:chunks], refs[chunks:]
     zb, refs = [refs[c * nz : (c + 1) * nz] for c in range(chunks)], refs[chunks * nz :]
     pk, refs = refs[:chunks], refs[chunks:]
     xr, refs = refs[:chunks], refs[chunks:]
-    ys, yr, zr, xv, one, loc = refs
+    er, yr, zr, xv, one, loc = refs
     hy, hz = ny // 2, nz // 2
     blocks = x_ref.shape[0] // BS
     half = blocks // 2
@@ -174,7 +174,8 @@
         dcat[0:cdim, i * BS : (i + 1) * BS] = piece
     for i in range(2, 6):
         loads[i].wait()
-    pinv = jnp.concatenate([pinv_ref[...], jnp.zeros((16 - nuis, BS), F32)], axis=0)
+    gap = jnp.zeros((EXTRA - nuis, BS), F32)
+    pinv = jnp.concatenate([pinv_ref[...], gap, gap, pinv_ref[...]], axis=0)
     for i, piece in enumerate(split3(pinv, True)):
         dcat[cdim : cdim + 16, i * BS : (i + 1) * BS] = piece
     for i, piece in enumerate(split3(x_ref[...], False)):
@@ -184,22 +185,28 @@
     load = lax.dot_general(ncat, dcat[0:cdim, :], NT, preferred_element_type=F32)
     for i in range(cdim // BS):
         mts[i] = load[0:EXTRA, i * BS : (i + 1) * BS]
+    far_dest = lax.rem(y + hy, ny)
+    first = jnp.concatenate(
+        [dcat[pl.ds(pl.multiple_of(far_dest * per_dest, per_dest), per_dest), :], dcat[cdim : cdim + 16, :]], axis=0)
     for b in range(0, blocks, 2):
-        both = lax.dot_general(dcat[...], xcat[b * BS : (b + 2) * BS, :], NT, preferred_element_type=F32)
-        for i in range(2):
-            mine = both[:, i * BS : (i + 1) * BS]
-            part[:, b + i] = mine[0:cdim].reshape(ny, per_dest, BS)
-            gpart[b + i] = mine[cdim : cdim + EXTRA]
+        both = lax.dot_general(first, xcat[b * BS : (b + 2) * BS, :], NT, preferred_element_type=F32)
+        for c in range(chunks):
+            for i in range(2):
+                sb[c][b + i] = both[c * rows : (c + 1) * rows, i * BS : (i + 1) * BS]
+        gpart[b // 2] = both[per_dest : per_dest + EXTRA, 0:BS] + both[per_dest + EXTRA :, BS : 2 * BS]
 
     def store_own(ref, dest, c, lo, hi, add):
         top = part[dest, lo:hi, c * rows : (c + 1) * rows, :]
         ref[lo:hi, 0:rows, :] = ref[lo:hi, 0:rows, :] + top if add else top
-        if c == 0:
-            more = gpart[lo:hi]
-            ref[lo:hi, rows : rows + EXTRA, :] = ref[lo:hi, rows : rows + EXTRA, :] + more if add else more
-            if lo == 0:
-                per = BS // per_dest
-                ref[0, rows : rows + EXTRA, :] = ref[0, rows : rows + EXTRA, :] + mts[dest // per]
+
+    et = gpart.shape[0] + 1
+    eh = et // 2
+    per = BS // per_dest
+
+    def store_extra(ref, dest, lo, hi, add):
+        for i in range(lo, hi):
+            value = gpart[i] if i < et - 1 else mts[dest // per]
+            ref[i] = ref[i] + value if add else value
 
     line = lax.broadcasted_iota(jnp.int32, (nz, BS), 0)
     place = lax.broadcasted_iota(jnp.int32, (nz, BS), 1)
@@ -215,19 +222,34 @@
     pl.semaphore_wait(barrier, len(peers))
 
     def step_s0(c, _):
-        store_own(sb[c], lax.rem(y + hy, ny), c, 0, blocks, False)
-        out = ys.at[min(c, 1)]
+        out = one.at[4]
+        if c == 0:
+            store_extra(es, far_dest, 0, et, False)
+            remote(es.at[0:eh], eb.at[0, 0:eh], one.at[5], er.at[0], y_dev(0))
+            remote(es.at[eh:et], eb.at[1, eh:et], one.at[5], er.at[0], y_dev(1))
         remote(sb[c].at[0:half], rb[c].at[0, 0:half], out, yr.at[c, 0], y_dev(0))
         remote(sb[c].at[half:blocks], rb[c].at[1, half:blocks], out, yr.at[c, 0], y_dev(1))
         if c == 0:
             for o in range(1, 8):
                 remote(req_ref, rq.at[m], one.at[2], one.at[3], x_dev(o))
 
+    def dest_of(s, d):
+        far = hy - 1 - s
+        return lax.rem(y + (far if d == 0 else ny - far), ny)
+
     def step_a(c, s):
+        if c == 0:
+            arrived(eb.at[0] if s == 0 else eb.at[0:2], er.at[s % 2])
+            for d in range(2):
+                held = eb.at[2 * s + d]
+                lo, hi = (0, et) if s else ((0, eh) if d == 0 else (eh, et))
+                store_extra(held, dest_of(s, d), lo, hi, True)
+                if s == 0:
+                    store_extra(held, dest_of(s, d), hi % et, lo if lo else et, False)
+                remote(held, eb.at[2 * s + 2 + d], one.at[5], er.at[(s + 1) % 2], y_dev(d))
         arrived(rb[c].at[0] if s == 0 else rb[c].at[0:2], yr.at[c, s % 2])
         for d in range(2):
-            far = hy - 1 - s
-            dest = lax.rem(y + (far if d == 0 else ny - far), ny)
+            dest = dest_of(s, d)
             held = rb[c].at[2 * s + d]
             if s == 0:
                 lo, hi = (0, half) if d == 0 else (half, blocks)
@@ -236,7 +258,7 @@
                 store_own(held, dest, c, other[0], other[1], False)
             else:
                 store_own(held, dest, c, 0, blocks, True)
-            remote(held, rb[c].at[2 * s + 2 + d], ys.at[min(c, 1)], yr.at[c, (s + 1) % 2], y_dev(d))
+            remote(held, rb[c].at[2 * s + 2 + d], one.at[4], yr.at[c, (s + 1) % 2], y_dev(d))
 
     def z_send(c, s, d):
         mine, theirs = ((nz - s) % nz, (nz - s - 1) % nz) if d == 0 else (s, s + 1)
@@ -276,12 +298,17 @@
         held = rb[c].at[2 * hy - 2]
         store_own(held, y, c, 0, blocks, True)
         if c == 0:
-            more = held[:, rows : rows + EXTRA, :] + rb[c][2 * hy - 1, :, rows : rows + EXTRA, :]
-            gfin[...] = more
-            square = jnp.concatenate([more[0], jnp.zeros((BS - EXTRA, BS), F32)], axis=0)
+            arrived(eb.at[0:2], er.at[(hy - 1) % 2])
+            last = eb.at[2 * hy - 2]
+            store_extra(last, y, 0, et, True)
+            for i in range(et - 1):
+                more = last[i] + eb[2 * hy - 1, i]
+                gfin[2 * i, 0:nuis, :] = more[0:nuis]
+                gfin[2 * i + 1, 0:nuis, :] = more[nuis : 2 * nuis]
+            square = jnp.concatenate(
+                [last[et - 1] + eb[2 * hy - 1, et - 1], jnp.zeros((BS - EXTRA, BS), F32)], axis=0)
             mcol[...] = jnp.transpose(square)
         total = held[:, 0:rows, :] + rb[c][2 * hy - 1, :, 0:rows, :]
-        per = BS // per_dest
         cols = mcol[pl.ds(lax.rem(y, per) * per_dest + c * rows, rows), :]
         for n in range(nuis):
             weight = jnp.broadcast_to(cols[:, nuis + n : nuis + n + 1], (rows, BS))
@@ -307,8 +334,8 @@
         for k in range(tv.shape[1]):
             tile = tv[b, k]
             high = tile.astype(BF16)
-            thi[b, :, k * BS : (k + 1) * BS] = high
-            tlo[b, :, k * BS : (k + 1) * BS] = (tile - high.astype(F32)).astype(BF16)
+            tcat[b, 0:BS, k * BS : (k + 1) * BS] = high
+            tcat[b, BS : 2 * BS, k * BS : (k + 1) * BS] = (tile - high.astype(F32)).astype(BF16)
 
     found = []
 
@@ -332,16 +359,22 @@
             value = jnp.concatenate(pieces, axis=1)
             high = value.astype(BF16).astype(F32)
             both = jnp.concatenate([high, value - high], axis=0).astype(BF16)
-            first = lax.dot_general(both, thi[b], NT, preferred_element_type=F32)
-            second = lax.dot_general(both, tlo[b], NT, preferred_element_type=F32)
-            out_ref[c * rows : (c + 1) * rows, b * BS : (b + 1) * BS] = (
-                first[0:rows] + (first[rows:] + second[0:rows]))
+            got = lax.dot_general(both, tcat[b], NT, preferred_element_type=F32)
+            out_ref[c * rows : (c + 1) * rows, b * BS : (b + 1) * BS] = got[0:rows, 0:BS] + (
+                got[rows:, 0:BS] + got[0:rows, BS:] + got[rows:, BS:])
 
     steps = dict(s0=step_s0, a=step_a, fin=step_fin, zf=step_zf, xp=step_xp, tp=step_tp, sm=step_sm)
+    for c in range(chunks):
+        step_s0(c, 0)
+    for b in range(0, blocks, 2):
+        both = lax.dot_general(dcat[0:cdim, :], xcat[b * BS : (b + 2) * BS, :], NT, preferred_element_type=F32)
+        for i in range(2):
+            part[:, b + i] = both[:, i * BS : (i + 1) * BS].reshape(ny, per_dest, BS)
     for name, which, step in plan(chunks, hy, hz, blocks, rows):
-        steps[name](which, step)
-    arrived(rb[0].at[0 : 2 * hy - 1], ys.at[0])
-    arrived(part.at[0 : 2 * hy - 1, :, rows:per_dest], ys.at[1])
+        if name != "s0":
+            steps[name](which, step)
+    arrived(part.at[0 : 2 * hy - 1], one.at[4])
+    arrived(eb.at[0 : 2 * hy - 1], one.at[5])
     arrived(part.at[0 : 2 * hz - 1], one.at[0])
     arrived(part.at[0:7], one.at[1])
     arrived(rq.at[0:7], one.at[2])
@@ -358,17 +391,19 @@
     chunks = per_dest // ROWS
     group = NX * NQ
     vm = pltpu.VMEM
-    rc = [ROWS + (EXTRA if c == 0 else 0) for c in range(chunks)]
-    hy, hz = ny // 2, nz // 2
+    rc = [ROWS] * chunks
+    hy = ny // 2
+    extra = blocks // 2 + 1
     sem = pltpu.SemaphoreType.DMA
     scratch = [
         vm(fixels.shape, F32), vm(perm_table.shape, jnp.int32), vm(contrast.shape, F32), vm(nuisance.shape, F32),
         vm(nuisance_pinv.shape, F32), vm((nz, BS), jnp.int32), pltpu.SMEM((tiles, blocks), jnp.int32),
         vm((cdim, BS), F32), vm((cdim + 16, 3 * BS), BF16), vm((fixel_count, 3 * BS), BF16),
-        vm((ny, blocks, per_dest, BS), F32), vm((blocks, EXTRA, BS), F32), vm((cdim // BS, EXTRA, BS), F32),
+        vm((ny, blocks, per_dest, BS), F32), vm((blocks // 2, EXTRA, BS), F32), vm((cdim // BS, EXTRA, BS), F32),
         vm((blocks, EXTRA, BS), F32), vm((BS, BS), F32),
-        vm(conn_tiles.shape, F32), vm((blocks, BS, tiles * BS), BF16), vm((blocks, BS, tiles * BS), BF16),
+        vm(conn_tiles.shape, F32), vm((blocks, 2 * BS, tiles * BS), BF16),
         vm((group, nz, BS), jnp.int32), pltpu.SMEM((group, nz, BS), jnp.int32),
+        vm((2 * hy, extra, EXTRA, BS), F32), vm((extra, EXTRA, BS), F32),
     ]
     scratch += [vm((blocks, r, BS), F32) for r in rc]
     scratch += [vm((2 * hy, blocks, r, BS), F32) for r in rc]
@@ -376,7 +411,7 @@
     scratch += [vm((group, nz, ROWS, BS), F32) for _ in rc]
     scratch += [vm((group, nz, ROWS, BS), F32) for _ in rc]
     scratch += [
-        sem((2,)), sem((chunks, 2)), sem((chunks, 2)), sem((chunks,)), sem((4,)), sem((8,)),
+        sem((2,)), sem((chunks, 2)), sem((chunks, 2)), sem((chunks,)), sem((6,)), sem((8,)),
     ]
     return pl.pallas_call(
         functools.partial(kernel, ny, nz, chunks),

time: 67.5 us -> 65.7 us (0.973)
  Pallas kernels: 65.7 us -> 63.9 us
    pallas_call x1, Pallas kernels: 65.7 us -> 63.9 us  [per_device(): pl.pallas_call(functools.partial(kernel, ny, nz, chunks), out_shape=jax.S...]
where the time goes in v5:
time: 65.7 us; the launch traced here: 65.6 us
  Pallas kernels  63.9 us (97%)
  local copies, waits for them, and re-layouts  1.67 us (3%)
    pallas_call x1, Pallas kernels, per_device(): pl.pallas_call(functools.partial(kernel, ny, nz, chunks), out_shape=jax.S...  63.9 us
    unnamed x1, local copies, waits for them, and re-layouts  1.67 us

profile of v5, /device:TPU:1, one launch (start us, length us, event | category | flops | bytes accessed | tf_op | source)
XLA Modules:
  0.0 65.6 jit_solution(12772684053120872991)
XLA Ops:
  0.0 63.9 %project_exchange.1 = f32[64,1024]{1,0:T(8,128)} custom-call(f32[1024,128]{1,0:T(8,128)} %refs_0_.1, f32[8,4,128,128]{3,2,1,0:T(8,128)} %refs_1_.1, s32[128,128]{1,0:T(8,128)} %refs_2_.1, f32[4,1024]{1,0:T(4,128)} %refs_3_.1, f32[4,128]{1,0:T(4,128)} %refs_4_.1, f32[4,128]{1,0:T(4,128)} %refs_5_.1, s32[4,8]{1,0:T(4,128)} %bitcast.1), custom_call_target="tpu_custom_call" | custom-call | tf_op jit(solution)/shard_map/project_exchange/pallas_call | solution.py:416
  63.9 1.7 %copy.9 = f32[64,1024]{1,0:T(8,128)} copy(f32[64,1024]{1,0:T(8,128)} %project_exchange.1) | data formatting | bytes 524288

commit v6 on v5

--- a/solution.py
+++ b/solution.py
@@ -56,7 +56,7 @@
             soonest = min(soonest, when)
         best = late if best is None else best
         if best is None:
-            if prepared < tiles and order:
+            if prepared < tiles and len(order) > 2 * chunks:
                 order.append(("tp", prepared, 0))
                 prepared += 1
                 t += cost["tp"]
@@ -147,7 +147,8 @@
         (pinv_hbm, pinv_ref), (col_hbm, col_ref), (t_ref, tv),
     )):
         loads.append(pltpu.make_async_copy(src, dst, loc.at[i]))
-        loads[-1].start()
+        if src is not t_ref:
+            loads[-1].start()
 
     def arrived(ref, sem):
         pltpu.make_async_copy(ref, ref, sem).wait()
@@ -185,6 +186,7 @@
     load = lax.dot_general(ncat, dcat[0:cdim, :], NT, preferred_element_type=F32)
     for i in range(cdim // BS):
         mts[i] = load[0:EXTRA, i * BS : (i + 1) * BS]
+    loads[6].start()
     far_dest = lax.rem(y + hy, ny)
     first = jnp.concatenate(
         [dcat[pl.ds(pl.multiple_of(far_dest * per_dest, per_dest), per_dest), :], dcat[cdim : cdim + 16, :]], axis=0)

time: 65.7 us -> 65.7 us (level)
  no operation moved by 1% of the time
where the time goes in v6:
time: 65.7 us; the launch traced here: 65.6 us
  Pallas kernels  63.9 us (97%)
  local copies, waits for them, and re-layouts  1.67 us (3%)
    pallas_call x1, Pallas kernels, per_device(): pl.pallas_call(functools.partial(kernel, ny, nz, chunks), out_shape=jax.S...  63.9 us
    unnamed x1, local copies, waits for them, and re-layouts  1.67 us

profile of v6, /device:TPU:1, one launch (start us, length us, event | category | flops | bytes accessed | tf_op | source)
XLA Modules:
  0.0 65.6 jit_solution(4902752233913438701)
XLA Ops:
  0.0 63.9 %project_exchange.1 = f32[64,1024]{1,0:T(8,128)} custom-call(f32[1024,128]{1,0:T(8,128)} %refs_0_.1, f32[8,4,128,128]{3,2,1,0:T(8,128)} %refs_1_.1, s32[128,128]{1,0:T(8,128)} %refs_2_.1, f32[4,1024]{1,0:T(4,128)} %refs_3_.1, f32[4,128]{1,0:T(4,128)} %refs_4_.1, f32[4,128]{1,0:T(4,128)} %refs_5_.1, s32[4,8]{1,0:T(4,128)} %bitcast.1), custom_call_target="tpu_custom_call" | custom-call | tf_op jit(solution)/shard_map/project_exchange/pallas_call | solution.py:418
  63.9 1.7 %copy.9 = f32[64,1024]{1,0:T(8,128)} copy(f32[64,1024]{1,0:T(8,128)} %project_exchange.1) | data formatting | bytes 524288

commit v7 on v5

--- a/solution.py
+++ b/solution.py
@@ -380,6 +380,17 @@
     arrived(rq.at[0:7], one.at[2])
 
 
+def write_out(held, out, done):
+    part = held.shape[0] // 4
+    copies = []
+    for i in range(4):
+        copies.append(pltpu.make_async_copy(
+            held.at[i * part : (i + 1) * part], out.at[i * part : (i + 1) * part], done.at[i]))
+        copies[-1].start()
+    for copy in copies:
+        copy.wait()
+
+
 def per_device(fixels, conn_tiles, columns, nuisance, nuisance_pinv, contrast, perm_table):
     ny = lax.axis_size("subj")
     nz = lax.axis_size("fix") // (NX * NQ)
@@ -413,7 +424,7 @@
     scratch += [
         sem((2,)), sem((chunks, 2)), sem((chunks, 2)), sem((chunks,)), sem((6,)), sem((8,)),
     ]
-    return pl.pallas_call(
+    held = pl.pallas_call(
         functools.partial(kernel, ny, nz, chunks),
         out_shape=jax.ShapeDtypeStruct((per_dest, fixel_count), F32),
         in_specs=[pl.BlockSpec(memory_space=pl.ANY)] * 7,
@@ -422,6 +433,14 @@
         compiler_params=pltpu.CompilerParams(collective_id=0, has_side_effects=True),
         name="project_exchange",
     )(fixels, conn_tiles, perm_table, contrast, nuisance, nuisance_pinv, columns.T)
+    return pl.pallas_call(
+        write_out,
+        out_shape=jax.ShapeDtypeStruct((per_dest, fixel_count), F32),
+        in_specs=[pl.BlockSpec(memory_space=pltpu.VMEM)],
+        out_specs=pl.BlockSpec(memory_space=pl.ANY),
+        scratch_shapes=[sem((4,))],
+        name="write_out",
+    )(held)
 
 
 def solution(mesh):

time: 65.7 us -> 65.7 us (level)
  Pallas kernels: 63.9 us -> 65.6 us
  local copies, waits for them, and re-layouts: 1.67 us -> 0 us
    pallas_call x0 -> x1, Pallas kernels: none -> 1.68 us  [per_device(): pl.pallas_call(write_out, out_shape=jax.ShapeDtypeStruct((per_dest, fixel...]
    unnamed x1 -> x0, local copies, waits for them, and re-layouts: 1.67 us -> none
where the time goes in v7:
time: 65.7 us; the launch traced here: 65.6 us
  Pallas kernels  65.6 us (100%)
    pallas_call x1, Pallas kernels, per_device(): pl.pallas_call(functools.partial(kernel, ny, nz, chunks), out_shape=jax.S...  63.9 us
    pallas_call x1, Pallas kernels, per_device(): pl.pallas_call(write_out, out_shape=jax.ShapeDtypeStruct((per_dest, fixel...  1.68 us

profile of v7, /device:TPU:1, one launch (start us, length us, event | category | flops | bytes accessed | tf_op | source)
XLA Modules:
  0.0 65.6 jit_solution(3607253951446822008)
XLA Ops:
  0.0 63.9 %project_exchange.1.held = f32[64,1024]{1,0:T(8,128)} custom-call(f32[1024,128]{1,0:T(8,128)} %refs_0_.1, f32[8,4,128,128]{3,2,1,0:T(8,128)} %refs_1_.1, s32[128,128]{1,0:T(8,128)} %refs_2_.1, f32[4,1024]{1,0:T(4,128)} %refs_3_.1, f32[4,128]{1,0:T(4,128)} %refs_4_.1, f32[4,128]{1,0:T(4,128)} %refs_5_.1, s32[4,8]{1,0:T(4,128)} %bitcast.1), custom_call_target="tpu_custom_call" | custom-call | tf_op jit(solution)/shard_map/project_exchange/pallas_call | solution.py:427
  63.9 1.7 %write_out.1 = f32[64,1024]{1,0:T(8,128)} custom-call(f32[64,1024]{1,0:T(8,128)} %project_exchange.1.held), custom_call_target="tpu_custom_call" | custom-call | tf_op jit(solution)/shard_map/write_out/pallas_call | solution.py:436
